TPU v7x, 32 devices: a whole 2x2x4 slice. The times are simulated.
32 devices in a mesh: role: 4 (over x, core), shard: 8 (over z, y).
Axes of the slice: x: 2, y: 2, z: 4, core: 2. Of those that a mesh axis runs over, the one named last changes fastest.
Arguments:
- action_ids: int32 [32, 8], P(('role', 'shard')), may hold values from 0 to 255
- traj_lengths: int32 [32], P(('role', 'shard')), may hold values from 1 to 8
- action_table: bfloat16 [256, 4096], P(None, 'shard'), may hold values from -6 to 6
- prefix_keys: bfloat16 [32, 128, 2048], P(('role', 'shard')), may hold values from -6 to 6
- prefix_values: bfloat16 [32, 128, 2048], P(('role', 'shard')), may hold values from -6 to 6
- qkv_weight: bfloat16 [4096, 6144], P('shard'), may hold values from -0.09375 to 0.09375
- out_weight: bfloat16 [2048, 4096], P(None, 'shard'), may hold values from -0.125 to 0.125
- first_qkv: float32 [4096, 6144], P('shard', 'role'), may hold values from -6 to 6
- second_qkv: float32 [4096, 6144], P('shard', 'role'), may hold values from 1 to 100
- first_out: float32 [2048, 4096], P('role', 'shard'), may hold values from -6 to 6
- second_out: float32 [2048, 4096], P('role', 'shard'), may hold values from 1 to 100
- out_cotangent: bfloat16 [256, 4096], P('role', 'shard'), may hold values from -6 to 6
Outputs:
- decoded: bfloat16 [256, 4096], P('role', 'shard')
- new_qkv: bfloat16 [4096, 6144], P('shard')
- new_out: bfloat16 [2048, 4096], P(None, 'shard')
- moment_qkv: float32 [4096, 6144], P('shard', 'role')
- square_qkv: float32 [4096, 6144], P('shard', 'role')
- moment_out: float32 [2048, 4096], P('role', 'shard')
- square_out: float32 [2048, 4096], P('role', 'shard')
All inputs are finite; a program needn't handle non-finite values.
Results may differ from a plain program's by a relative error of at most 0.0071.
Values may be sent and summed in bfloat16 or wider, within the bound.
No kernel may reach another device: no remote copies, remote signals or barrier semaphores. Data moves between devices by JAX's collectives and lax.ppermute only.
A program may use at most 128 MiB of HBM per device.

v0:
```python
import functools

import jax
import jax.numpy as jnp
from jax import lax
from jax.experimental import pallas as pl
from jax.experimental.pallas import tpu as pltpu
from jax.sharding import PartitionSpec as P


HD = 128


learn_rate = 0.001
first_decay = 0.9
second_decay = 0.95
adam_eps = 1e-08
weight_decay = 0.1
first_fix = 1.0 - 0.9**10
second_fix = 1.0 - 0.95**10


def unpack(qkv_rows, keys_pre, vals_pre):
    span_width = keys_pre.shape[-1]
    head_count = span_width // HD
    positions = qkv_rows.shape[0]
    total_keys = keys_pre.shape[0] + positions
    queries = qkv_rows[:, :span_width].astype(jnp.float32).reshape(positions, head_count, HD)
    all_keys = (
        jnp.concatenate([keys_pre, qkv_rows[:, span_width : 2 * span_width]], 0)
        .astype(jnp.float32)
        .reshape(total_keys, head_count, HD)
    )
    all_values = (
        jnp.concatenate([vals_pre, qkv_rows[:, 2 * span_width :]], 0)
        .astype(jnp.float32)
        .reshape(total_keys, head_count, HD)
    )
    return (queries, all_keys, all_values)


def attend(qkv_rows, keys_pre, vals_pre, length):
    queries, all_keys, all_values = unpack(qkv_rows, keys_pre, vals_pre)
    prefix_len = keys_pre.shape[0]
    positions = qkv_rows.shape[0]
    attn_scale = HD ** (-0.5)
    scores = jnp.einsum("thd,lhd->htl", queries, all_keys) * attn_scale
    position = jnp.arange(positions, dtype=jnp.int32)[:, None]
    offset = jnp.arange(prefix_len + positions, dtype=jnp.int32)[None, :] - prefix_len
    allowed = (offset < 0) | (offset <= position) & (offset < length)
    scores = jnp.where(allowed[None], scores, -1e30)
    weights = jax.nn.softmax(scores, axis=-1)
    rounded = lax.optimization_barrier(weights.astype(jnp.bfloat16))
    head_mix = jnp.einsum("htl,lhd->thd", rounded.astype(jnp.float32), all_values)
    return (head_mix.reshape(positions, -1).astype(jnp.bfloat16), weights, rounded)


def attend_back(qkv_rows, keys_pre, vals_pre, weights, rounded, upstream):
    queries, all_keys, all_values = unpack(qkv_rows, keys_pre, vals_pre)
    prefix_len = keys_pre.shape[0]
    positions = qkv_rows.shape[0]
    attn_scale = HD ** (-0.5)
    grads_head = upstream.astype(jnp.float32).reshape(positions, -1, HD)
    grad_weights = jnp.einsum("thd,lhd->htl", grads_head, all_values)
    grad_scores = (
        weights
        * (grad_weights - jnp.sum(weights * grad_weights, axis=-1, keepdims=True))
        * attn_scale
    )
    grad_rounded = lax.optimization_barrier(grad_scores.astype(jnp.bfloat16)).astype(jnp.float32)
    grad_query = jnp.einsum("htl,lhd->thd", grad_rounded, all_keys).reshape(positions, -1)
    grad_key = jnp.einsum("htl,thd->lhd", grad_rounded[:, :, prefix_len:], queries).reshape(
        positions, -1
    )
    grad_value = jnp.einsum(
        "htl,thd->lhd", rounded.astype(jnp.float32)[:, :, prefix_len:], grads_head
    ).reshape(positions, -1)
    return jnp.concatenate([grad_query, grad_key, grad_value], 1).astype(jnp.bfloat16)


def pack_body(first_ref, second_ref, out_ref):
    width = out_ref.shape[1] // 2
    out_ref[:, :width] = first_ref[...].astype(out_ref.dtype)
    out_ref[:, width:] = second_ref[...].astype(out_ref.dtype)


def pack(first, second, width):
    depth = first.shape[0]
    steps = 2
    spec = pl.BlockSpec((depth // steps, width), lambda i: (i, 0))
    return pl.pallas_call(
        pack_body,
        grid=(steps,),
        in_specs=[spec, spec],
        out_specs=pl.BlockSpec((depth // steps, 2 * width), lambda i: (i, 0)),
        out_shape=jax.ShapeDtypeStruct((depth, 2 * width), jnp.bfloat16),
        cost_estimate=pl.CostEstimate(flops=0, bytes_accessed=12 * depth * width, transcendentals=0),
        name="pack",
    )(first, second)


def stack_body(edges, *refs):
    count = len(refs) - len(edges) + 1
    rows = refs[0].shape[0]
    for i in range(count):
        for j, out in enumerate(refs[count:]):
            out[i * rows : (i + 1) * rows, :] = refs[i][:, edges[j] : edges[j + 1]]


def stack(blocks, cuts):
    edges = [sum(cuts[:i]) for i in range(len(cuts) + 1)]
    height = len(blocks) * blocks[0].shape[0]
    return pl.pallas_call(
        functools.partial(stack_body, edges),
        out_shape=[jax.ShapeDtypeStruct((height, c), blocks[0].dtype) for c in cuts],
        name="stack",
    )(*blocks)


def parcel_body(plan, *refs):
    outs = refs[-len(plan) :]
    for out, takes in zip(outs, plan):
        at = 0
        for which, begin, end in takes:
            out[:, at : at + end - begin] = refs[which][:, begin:end]
            at += end - begin


def parcel(sources, plan):
    return pl.pallas_call(
        functools.partial(parcel_body, plan),
        out_shape=[
            jax.ShapeDtypeStruct(
                (sources[0].shape[0], sum(e - b for _, b, e in takes)), sources[0].dtype
            )
            for takes in plan
        ],
        name="parcel",
    )(*sources)


def adamw_folded(params, gradient, first_moment, second_moment):
    moment_one = first_decay * first_moment + (1.0 - first_decay) * gradient
    moment_two = second_decay * second_moment + (1.0 - second_decay) * gradient * gradient
    fixed = moment_two * (1.0 / second_fix)
    stepped = (moment_one * (learn_rate / first_fix)) / (fixed * lax.rsqrt(fixed) + adam_eps)
    updated = params.astype(jnp.float32) * (1.0 - learn_rate * weight_decay) - stepped
    return (updated, moment_one, moment_two)


def update_body(aliased, role_ref, left_ref, right_ref, w_ref, m_ref, v_ref, *refs):
    grad_ref = refs[-1]
    outs = refs[aliased:-1]
    grad_ref[...] = lax.dot_general(
        left_ref[...], right_ref[...], (((0,), (0,)), ((), ())), preferred_element_type=jnp.float32
    )
    strip = 16

    def one(i, carry):
        at = pl.ds(pl.multiple_of(i * strip, strip), strip)
        updated, moment, square = adamw_folded(
            w_ref[at, :],
            grad_ref[at, :],
            m_ref[at, :].astype(jnp.float32),
            v_ref[at, :].astype(jnp.float32),
        )
        outs[0][at, :] = updated.astype(outs[0].dtype)
        if len(outs) > 1:
            outs[1][at, :] = moment
            outs[2][at, :] = square
        return carry

    lax.fori_loop(0, w_ref.shape[0] // strip, one, 0, unroll=2)


def update_blocks(role, left, right, weight, first, second, spots, shape, block, moments=None, keep=True):
    height, width = block
    grid = (shape[0] // height, shape[1] // width)
    depth = left.shape[0]
    at = {k: (lambda f: lambda i, j, p: f(i, j))(f) for k, f in spots.items() if k != "weight"}
    in_specs = [
        pl.BlockSpec((depth, height), at["left"]),
        pl.BlockSpec((depth, width), at["right"]),
        pl.BlockSpec(block, lambda i, j, p: spots["weight"](i, j, p[0])),
        pl.BlockSpec(block, at["first"]),
        pl.BlockSpec(block, at["second"]),
    ]
    out_specs = [pl.BlockSpec(block, lambda i, j, p: (i, j))]
    out_shape = [jax.ShapeDtypeStruct(shape, jnp.bfloat16)]
    operands = [left, right, weight, first, second]
    aliases = {}
    if keep:
        out_specs += [pl.BlockSpec(block, at["first"])] * 2
        out_shape += [jax.ShapeDtypeStruct(first.shape, jnp.float32)] * 2
        if moments is not None:
            operands += list(moments)
            in_specs += [pl.BlockSpec(memory_space=pl.ANY)] * 2
            aliases = {6: 1, 7: 2}
    size = shape[0] * shape[1]
    return pl.pallas_call(
        functools.partial(update_body, len(aliases)),
        grid_spec=pltpu.PrefetchScalarGridSpec(
            num_scalar_prefetch=1,
            grid=grid,
            in_specs=in_specs,
            out_specs=out_specs,
            scratch_shapes=[pltpu.VMEM(block, jnp.float32)],
        ),
        out_shape=out_shape,
        input_output_aliases=aliases,
        cost_estimate=pl.CostEstimate(
            flops=2 * depth * size, bytes_accessed=(20 if keep else 8) * size, transcendentals=2 * size
        ),
        name="update",
    )(role.reshape(1).astype(jnp.int32), *operands)


def join_body(role_ref, *refs):
    roles = refs[-1].shape[0]
    early, late, outs = refs[:roles], refs[roles : 2 * roles], refs[2 * roles : 3 * roles]
    qkv_ref, out_ref = refs[-2:]
    first, rest = early[0].shape[1], late[0].shape[1]
    for d in range(roles):
        owner = role_ref[0] ^ d
        qkv_ref[:, pl.ds(pl.multiple_of(owner * (first + rest), 128), first)] = early[d][...]
        qkv_ref[:, pl.ds(pl.multiple_of(owner * (first + rest) + first, 128), rest)] = late[d][...]
        out_ref[owner] = outs[d][...]


def join(role, early, late, outs):
    roles = len(outs)
    depth = early[0].shape[0]
    width = early[0].shape[1] + late[0].shape[1]
    out_rows, out_width = outs[0].shape
    steps = 2
    pieces = [*early, *late, *outs]
    new_qkv, new_out = pl.pallas_call(
        join_body,
        grid=(steps,),
        in_specs=[pl.BlockSpec(memory_space=pltpu.SMEM)]
        + [pl.BlockSpec((x.shape[0] // steps, x.shape[1]), lambda i: (i, 0)) for x in pieces],
        out_specs=[
            pl.BlockSpec((depth // steps, roles * width), lambda i: (i, 0)),
            pl.BlockSpec((roles, out_rows // steps, out_width), lambda i: (0, i, 0)),
        ],
        out_shape=[
            jax.ShapeDtypeStruct((depth, roles * width), jnp.bfloat16),
            jax.ShapeDtypeStruct((roles, out_rows, out_width), jnp.bfloat16),
        ],
        cost_estimate=pl.CostEstimate(
            flops=0, bytes_accessed=4 * roles * (depth * width + out_rows * out_width), transcendentals=0
        ),
        name="join",
    )(role.reshape(1).astype(jnp.int32), *pieces)
    return new_qkv, new_out.reshape(roles * out_rows, out_width)


def update(
    action_ids,
    traj_lengths,
    action_table,
    prefix_keys,
    prefix_values,
    qkv_weight,
    out_weight,
    first_qkv,
    second_qkv,
    first_out,
    second_out,
    out_cotangent,
):
    f32, bf16 = jnp.float32, jnp.bfloat16
    episodes, horizon = action_ids.shape
    rows = episodes * horizon
    roles, parts = lax.axis_size("role"), lax.axis_size("shard")
    role, part = lax.axis_index("role"), lax.axis_index("shard")
    learner = roles - 1
    is_learner = role == learner
    far = roles // 2
    qkv_part = first_qkv.shape[1]
    out_part = first_out.shape[0]
    head_width = prefix_keys.shape[-1]
    early_width = qkv_part // 3 * 2

    def hop(x, k):
        return lax.ppermute(x, "shard", [(i, i ^ k) for i in range(parts)])

    def gather_turned(x):
        return jnp.concatenate([x] + [hop(x, k) for k in range(1, parts)], 0)

    spot = jnp.arange(parts * rows, dtype=jnp.int32)
    turn_matrix = ((spot[:, None] ^ (part * rows)) == spot[None, :]).astype(bf16)

    def turn(x):
        return jnp.dot(turn_matrix, x, preferred_element_type=f32).astype(x.dtype)

    def swap(x, bit):
        return lax.ppermute(x, "role", [(i, i ^ bit) for i in range(roles)])

    far_moments = swap(pack(first_qkv, second_qkv, early_width), far)

    ids = gather_turned(action_ids)

    turned_cot = turn(out_cotangent)
    grad_partial = lax.dot_general(
        turned_cot, out_weight, (((1,), (1,)), ((), ())), preferred_element_type=f32
    )

    def inputs_of(bins):
        onehot = (
            bins.reshape(-1)[:, None] == jnp.arange(action_table.shape[0], dtype=jnp.int32)[None, :]
        ).astype(bf16)
        return jnp.dot(onehot, action_table, preferred_element_type=f32).astype(bf16)

    partial = jnp.concatenate(
        [jnp.dot(inputs_of(ids), qkv_weight, preferred_element_type=f32), grad_partial], 1
    )
    total = partial[:rows]
    pieces = partial[rows:].astype(bf16)
    for k in range(1, parts):
        total = total + hop(pieces[(k - 1) * rows : k * rows], k).astype(f32)
    total = total.astype(bf16)

    near_cot = jnp.where(is_learner, turned_cot, swap(turned_cot, 1))
    learner_cot = jnp.where(role >= far, near_cot, swap(near_cot, far))

    projected = total[:, : 3 * head_width].reshape(episodes, horizon, -1)
    grad_heads = total[:, 3 * head_width :]
    head_mix, weights, rounded = jax.vmap(attend)(
        projected, prefix_keys, prefix_values, traj_lengths
    )
    head_rows = head_mix.reshape(rows, -1)
    valid = (jnp.arange(horizon, dtype=jnp.int32)[None, :] < traj_lengths[:, None]).reshape(-1)
    grad_heads = jnp.where(valid[:, None], grad_heads, jnp.zeros_like(grad_heads))
    masked_rows = jnp.where(valid[:, None], head_rows, jnp.zeros_like(head_rows))
    grad_proj = jax.vmap(attend_back)(
        projected,
        prefix_keys,
        prefix_values,
        weights,
        rounded,
        grad_heads.reshape(episodes, horizon, -1),
    ).reshape(rows, -1)

    id_column = jnp.broadcast_to(action_ids.reshape(rows, 1).astype(bf16), (rows, 128))

    def wanted(q):
        own, other = q * qkv_part, (q ^ far) * qkv_part
        return (
            (0, own, own + qkv_part),
            (0, other, other + early_width),
            (1, q * out_part, (q + 1) * out_part),
            (1, (q ^ far) * out_part, ((q ^ far) + 1) * out_part),
            (2, 0, 128),
        )

    parcels = parcel([grad_proj, masked_rows, id_column], tuple(wanted(q) for q in range(roles)))
    mine = None
    for q in range(learner):
        got = lax.ppermute(parcels[q], "role", [(learner, q)])
        mine = got if mine is None else mine + got
    mine = jnp.where(is_learner, parcels[learner], mine)
    mine = jnp.concatenate([mine, head_rows], 1)
    moments_out = jnp.concatenate([first_out.astype(bf16), second_out.astype(bf16)], 0)
    far_moments_out = swap(moments_out, far)
    blocks = [mine] + [hop(mine, k) for k in range(1, parts)]
    cuts = [qkv_part, early_width, out_part, out_part, 128, head_width]
    own_rows, far_rows, own_mixed, far_mixed, learner_ids, gathered = stack(blocks, cuts)
    learner_inputs = inputs_of(learner_ids[:, 0].astype(jnp.int32))

    third = qkv_part - early_width
    high = min(256, first_qkv.shape[0])

    def spots(at, moved, weight):
        return {
            "left": lambda i, j: (0, i),
            "right": lambda i, j: (0, at + j),
            "first": lambda i, j: (i, at + j),
            "second": lambda i, j: (i, at + j + moved),
            "weight": weight,
        }

    late, moment_qkv, square_qkv = update_blocks(
        role, learner_inputs, own_rows, qkv_weight, first_qkv, second_qkv,
        spots(2, 0, lambda i, j, r: (i, r * 3 + 2 + j)), (first_qkv.shape[0], third), (high, third),
    )
    far_late = swap(late, far)
    near_late = swap(late, 1)
    piece_qkv, moment_qkv, square_qkv = update_blocks(
        role, learner_inputs, own_rows, qkv_weight, first_qkv, second_qkv,
        spots(0, 0, lambda i, j, r: (i, r * 3 + j)), (first_qkv.shape[0], early_width), (high, third),
        moments=(moment_qkv, square_qkv),
    )
    late_done = late
    (piece_far,) = update_blocks(
        role, learner_inputs, far_rows, qkv_weight, far_moments, far_moments,
        spots(0, 2, lambda i, j, r: (i, (r ^ far) * 3 + j)), (first_qkv.shape[0], early_width), (high, third), keep=False,
    )
    near_far = swap(piece_far, 1)
    tall = min(256, out_part)
    stories = out_part // tall
    (far_out,) = update_blocks(
        role, far_mixed, learner_cot, out_weight, far_moments_out, far_moments_out,
        {
            **spots(0, 0, lambda i, j, r: ((r ^ far) * stories + i, j)),
            "second": lambda i, j: (i + stories, j),
        },
        (out_part, first_out.shape[1]), (tall, first_out.shape[1]), keep=False,
    )
    piece_out, moment_out, square_out = update_blocks(
        role, own_mixed, learner_cot, out_weight, first_out, second_out,
        spots(0, 0, lambda i, j, r: (r * stories + i, j)), (out_part, first_out.shape[1]), (tall, first_out.shape[1]),
    )
    near_qkv = swap(piece_qkv, 1)
    near_out = swap(piece_out, 1)
    near_far_out = swap(far_out, 1)
    diagonal_late = swap(far_late, 1)
    new_qkv, new_out = join(
        role,
        [piece_qkv, near_qkv, piece_far, near_far],
        [late_done, near_late, far_late, diagonal_late],
        [piece_out, near_out, far_out, near_far_out],
    )

    decoded = turn(jnp.dot(gathered, out_weight, preferred_element_type=f32).astype(bf16))
    return (decoded, new_qkv, new_out, moment_qkv, square_qkv, moment_out, square_out)


def solution(mesh):
    in_specs = (
        P(("role", "shard"), None),
        P(("role", "shard")),
        P(None, "shard"),
        P(("role", "shard"), None, None),
        P(("role", "shard"), None, None),
        P("shard", None),
        P(None, "shard"),
        P("shard", "role"),
        P("shard", "role"),
        P("role", "shard"),
        P("role", "shard"),
        P("role", "shard"),
    )
    out_specs = (
        P("role", "shard"),
        P("shard", None),
        P(None, "shard"),
        P("shard", "role"),
        P("shard", "role"),
        P("role", "shard"),
        P("role", "shard"),
    )
    return jax.shard_map(update, mesh=mesh, in_specs=in_specs, out_specs=out_specs, check_vma=False)
```

profile of v0, /device:TPU:0, one launch (start us, length us, event | category | flops | bytes accessed | tf_op | source)
XLA Modules:
  0.0 162.7 jit_solution(1678499201241458338)
XLA Ops:
  0.7 6.1 %collective-permute-start.6 = (s32[1,8]{1,0:T(1,128)}, s32[1,8]{1,0:T(1,128)S(1)}, u32[]{:S(2)}, u32[]{:S(2)}) collective-permute-start(s32[1,8]{1,0:T(1,128)} %param.12), channel_id=1, source_target_pairs={{0,7},{1,6},{2,5},{3,4},{4,3},{5,2},{6,1},{7,0},{8,15},{9,14},{10,... | collective-permute-start | bytes 104 | tf_op jit(solution)/shard_map/ppermute | solution.py:286
  7.0 0.7 collective-permute-start.4
  7.7 2.0 %collective-permute-start.3 = (s32[1,8]{1,0:T(1,128)}, s32[1,8]{1,0:T(1,128)S(1)}, u32[]{:S(2)}, u32[]{:S(2)}) collective-permute-start(s32[1,8]{1,0:T(1,128)} %param.12), channel_id=1, source_target_pairs={{0,4},{1,5},{2,6},{3,7},{4,0},{5,1},{6,2},{7,3},{8,12},{9,13},{10,... | collective-permute-start | bytes 104 | tf_op jit(solution)/shard_map/ppermute | solution.py:286
  9.8 2.3 %collective-permute-start.2 = (s32[1,8]{1,0:T(1,128)}, s32[1,8]{1,0:T(1,128)S(1)}, u32[]{:S(2)}, u32[]{:S(2)}) collective-permute-start(s32[1,8]{1,0:T(1,128)} %param.12), channel_id=1, source_target_pairs={{0,3},{1,2},{2,1},{3,0},{4,7},{5,6},{6,5},{7,4},{8,11},{9,10},{10,... | collective-permute-start | bytes 104 | tf_op jit(solution)/shard_map/ppermute | solution.py:286
  12.7 1.0 convolution_convert_fusion.2
  13.8 2.3 %fusion.57 = f32[64,2048]{1,0:T(8,128)S(1)} fusion(bf16[64,512]{1,0:T(8,128)(2,1)S(1)} %convolution_convert_fusion.2, bf16[2048,512]{1,0:T(8,128)(2,1)} %w_ref.9), kind=kOutput, calls=%fused_computation.88 | convolution fusion | flops 134217728 | bytes 2686976 | tf_op jit(solution)/shard_map/dot_general | solution.py:305
  16.1 0.8 collective-permute-start.1
  17.4 2.4 %collective-permute-done.1 = s32[1,8]{1,0:T(1,128)S(1)} collective-permute-done((s32[1,8]{1,0:T(1,128)S(1)}, s32[1,8]{1,0:T(1,128)S(1)}, u32[]{:S(2)}, u32[]{:S(2)}) %collective-permute-start.1) | collective-permute-done | bytes 64 | tf_op jit(solution)/shard_map/ppermute | solution.py:286
  19.8 0.8 collective-permute-done
  20.7 4.2 %fusion.12 = f32[64,6144]{1,0:T(8,128)S(1)} fusion(bf16[512,6144]{1,0:T(8,128)(2,1)} %w_ref.7, bf16[256,512]{1,0:T(8,128)(2,1)S(1)} %copy-done, s32[64]{0:T(128)S(1)} %eq.53), kind=kOutput, calls=%fused_computation.21 | convolution fusion | flops 419479552 | bytes 8126720 | tf_op jit(solution)/shard_map/dot_general | solution.py:316
  25.0 0.8 fusion.51
  26.2 4.6 %collective-permute-start.13 = (bf16[8,8192]{1,0:T(8,128)(2,1)S(1)}, bf16[8,8192]{1,0:T(8,128)(2,1)S(1)}, u32[]{:S(2)}, u32[]{:S(2)}) collective-permute-start(bf16[8,8192]{1,0:T(8,128)(2,1)S(1)} %get-tuple-element.50), channel_id=1, source_target_pairs={{0,7},{1,6},{2,5},{3,4},{4,3},{5,2},{6,1},{7,0},{8,15},{9,14},{10,... | collective-permute-start | bytes 393224 | tf_op jit(solution)/shard_map/ppermute | solution.py:286
  31.5 2.4 %collective-permute-start.10 = (bf16[8,8192]{1,0:T(8,128)(2,1)}, bf16[8,8192]{1,0:T(8,128)(2,1)}, u32[]{:S(2)}, u32[]{:S(2)}) collective-permute-start(bf16[8,8192]{1,0:T(8,128)(2,1)} %get-tuple-element.53), channel_id=1, source_target_pairs={{0,4},{1,5},{2,6},{3,7},{4,0},{5,1},{6,2},{7,3},{8,12},{9,13},{10,... | collective-permute-start | bytes 393224 | tf_op jit(solution)/shard_map/ppermute | solution.py:286
  33.9 2.3 %collective-permute-start.9 = (bf16[8,8192]{1,0:T(8,128)(2,1)}, bf16[8,8192]{1,0:T(8,128)(2,1)}, u32[]{:S(2)}, u32[]{:S(2)}) collective-permute-start(bf16[8,8192]{1,0:T(8,128)(2,1)} %get-tuple-element.54), channel_id=1, source_target_pairs={{0,3},{1,2},{2,1},{3,0},{4,7},{5,6},{6,5},{7,4},{8,11},{9,10},{10,... | collective-permute-start | bytes 393224 | tf_op jit(solution)/shard_map/ppermute | solution.py:286
  36.9 7.8 %collective-permute-start.8 = (bf16[8,8192]{1,0:T(8,128)(2,1)}, bf16[8,8192]{1,0:T(8,128)(2,1)}, u32[]{:S(2)}, u32[]{:S(2)}) collective-permute-start(bf16[8,8192]{1,0:T(8,128)(2,1)} %get-tuple-element.55), channel_id=1, source_target_pairs={{0,2},{1,3},{2,0},{3,1},{4,6},{5,7},{6,4},{7,5},{8,10},{9,11},{10,... | collective-permute-start | bytes 393224 | tf_op jit(solution)/shard_map/ppermute | solution.py:286
  44.7 0.9 convert_element_type.126
  46.2 3.3 %pack.1 = bf16[512,2048]{1,0:T(8,128)(2,1)} custom-call(f32[512,1536]{1,0:T(8,128)} %first_ref.1, f32[512,1536]{1,0:T(8,128)} %second_ref.1), custom_call_target="tpu_custom_call" | custom-call | bytes 6291456 | tf_op jit(solution)/shard_map/pack/pallas_call | solution.py:91
  49.5 1.6 collective-permute-start.25
  51.3 1.4 fusion.31
  55.6 0.7 pad_maximum_fusion.2.refs_0_
  56.2 0.9 broadcast_select_fusion.2
  57.7 1.6 parcel.1
  59.4 1.3 collective-permute-start.14
  60.6 0.7 collective-permute-start.15
  61.3 0.7 collective-permute-start.16
  62.0 1.6 collective-permute-start.31
  63.6 34.9 %collective-permute-done.14 = bf16[8,3712]{1,0:T(8,128)(2,1)S(1)} collective-permute-done((bf16[8,3712]{1,0:T(8,128)(2,1)}, bf16[8,3712]{1,0:T(8,128)(2,1)S(1)}, u32[]{:S(2)}, u32[]{:S(2)}) %collective-permute-start.14) | collective-permute-done | bytes 59424 | tf_op jit(solution)/shard_map/ppermute | solution.py:360
  98.6 3.6 %collective-permute-start.23 = (bf16[8,5760]{1,0:T(8,128)(2,1)S(1)}, bf16[8,5760]{1,0:T(8,128)(2,1)S(1)}, u32[]{:S(2)}, u32[]{:S(2)}) collective-permute-start(bf16[8,5760]{1,0:T(8,128)(2,1)S(1)} %pad_maximum_fusion.3.refs_0_), channel_id=1, source_target_pairs={{0,7},{1,6},{2,5},{3,4},{4,3},{5,2},{6,1},{7,0},{8,15},{9,14},{10,... | collective-permute-start | bytes 276488 | tf_op jit(solution)/shard_map/ppermute | solution.py:286
  102.2 1.1 collective-permute-start.22
  103.3 3.0 %collective-permute-start.20 = (bf16[8,5760]{1,0:T(8,128)(2,1)S(1)}, bf16[8,5760]{1,0:T(8,128)(2,1)S(1)}, u32[]{:S(2)}, u32[]{:S(2)}) collective-permute-start(bf16[8,5760]{1,0:T(8,128)(2,1)S(1)} %pad_maximum_fusion.3.refs_0_), channel_id=1, source_target_pairs={{0,4},{1,5},{2,6},{3,7},{4,0},{5,1},{6,2},{7,3},{8,12},{9,13},{10,... | collective-permute-start | bytes 276488 | tf_op jit(solution)/shard_map/ppermute | solution.py:286
  106.6 2.9 %collective-permute-done.22.refs_6_ = bf16[8,5760]{1,0:T(8,128)(2,1)S(1)} collective-permute-done((bf16[8,5760]{1,0:T(8,128)(2,1)S(1)}, bf16[8,5760]{1,0:T(8,128)(2,1)S(1)}, u32[]{:S(2)}, u32[]{:S(2)}) %collective-permute-start.22) | collective-permute-done | bytes 92192 | tf_op jit(solution)/shard_map/ppermute | solution.py:286
  109.6 5.1 %collective-permute-start.19 = (bf16[8,5760]{1,0:T(8,128)(2,1)S(1)}, bf16[8,5760]{1,0:T(8,128)(2,1)S(1)}, u32[]{:S(2)}, u32[]{:S(2)}) collective-permute-start(bf16[8,5760]{1,0:T(8,128)(2,1)S(1)} %pad_maximum_fusion.3.refs_0_), channel_id=1, source_target_pairs={{0,3},{1,2},{2,1},{3,0},{4,7},{5,6},{6,5},{7,4},{8,11},{9,10},{10,... | collective-permute-start | bytes 276488 | tf_op jit(solution)/shard_map/ppermute | solution.py:286
  114.7 1.4 collective-permute-done.21.refs_5_
  116.1 2.1 %collective-permute-done.20.refs_4_ = bf16[8,5760]{1,0:T(8,128)(2,1)S(1)} collective-permute-done((bf16[8,5760]{1,0:T(8,128)(2,1)S(1)}, bf16[8,5760]{1,0:T(8,128)(2,1)S(1)}, u32[]{:S(2)}, u32[]{:S(2)}) %collective-permute-start.20) | collective-permute-done | bytes 92192 | tf_op jit(solution)/shard_map/ppermute | solution.py:286
  119.4 0.9 collective-permute-done.19.refs_3_
  120.3 1.9 %collective-permute-done.18.refs_2_ = bf16[8,5760]{1,0:T(8,128)(2,1)S(1)} collective-permute-done((bf16[8,5760]{1,0:T(8,128)(2,1)S(1)}, bf16[8,5760]{1,0:T(8,128)(2,1)S(1)}, u32[]{:S(2)}, u32[]{:S(2)}) %collective-permute-start.18) | collective-permute-done | bytes 92192 | tf_op jit(solution)/shard_map/ppermute | solution.py:286
  122.2 0.8 collective-permute-done.17.refs_1_
  123.7 2.1 %stack.1 = (bf16[64,1536]{1,0:T(8,128)(2,1)}, bf16[64,1024]{1,0:T(8,128)(2,1)}, bf16[64,512]{1,0:T(8,128)(2,1)}, bf16[64,512]{1,0:T(8,128)(2,1)}, bf16[64,128]{1,0:T(8,128)(2,1)}, /*index=5*/bf16[64,2048]{1,0:T(8,128)(2,1)}) custom-call(bf16[8,5760]{1,0:T(8,128)(2,1)} %copy-done.11, bf16[8,5760]{1,0:T(8,128)(2,1)} %copy-done.20, bf16[8,5760]{1,0:T(8,128)(2,1)} %copy-done.19, ...), custom_call_target="tpu_custom_call" | custom-call | tf_op jit(solution)/shard_map/stack/pallas_call | solution.py:113
  125.8 3.8 %update.8 = (bf16[512,512]{1,0:T(8,128)(2,1)}, f32[512,512]{1,0:T(8,128)}, f32[512,512]{1,0:T(8,128)}) custom-call(s32[1]{0:T(128)} %bitcast.23.role_ref, bf16[64,512]{1,0:T(8,128)(2,1)} %get-tuple-element.40.left_ref, bf16[64,512]{1,0:T(8,128)(2,1)} %broadcast_select_fusion.1.right_ref, bf16[2048,512]{1,0:T(8,128)(2,1)} %w_ref.9, f32[512,512]{1,0:T(8,128)} %m_ref.5, ...), custom_call_target="tpu_custom_call" | custom-call | flops 33554432 | bytes 5242880 | tf_op jit(solution)/shard_map/update/pallas_call | solution.py:200
  129.7 0.9 convolution_convert_fusion.3.left_ref
  130.5 3.8 %update.5 = (bf16[512,512]{1,0:T(8,128)(2,1)}, f32[512,1536]{1,0:T(8,128)}, f32[512,1536]{1,0:T(8,128)}) custom-call(s32[1]{0:T(128)} %bitcast.23.role_ref, bf16[64,512]{1,0:T(8,128)(2,1)} %convolution_convert_fusion.3.left_ref, bf16[64,1536]{1,0:T(8,128)(2,1)} %get-tuple-element.34.right_ref, bf16[512,6144]{1,0:T(8,128)(2,1)} %w_ref.7, ...), custom_call_target="tpu_custom_call" | custom-call | flops 33554432 | bytes 5242880 | tf_op jit(solution)/shard_map/update/pallas_call | solution.py:200
  134.3 6.8 %update.6 = (bf16[512,1024]{1,0:T(8,128)(2,1)}, f32[512,1536]{1,0:T(8,128)}, f32[512,1536]{1,0:T(8,128)}) custom-call(s32[1]{0:T(128)} %bitcast.23.role_ref, bf16[64,512]{1,0:T(8,128)(2,1)} %convolution_convert_fusion.3.left_ref, bf16[64,1536]{1,0:T(8,128)(2,1)} %get-tuple-element.34.right_ref, ...), custom_call_target="tpu_custom_call", output_to_operand_aliasing={{1}: (6, {}), {2}: (7, {})} | custom-call | flops 67108864 | bytes 10485760 | tf_op jit(solution)/shard_map/update/pallas_call | solution.py:200
  141.6 5.3 %update.7.refs_2_ = bf16[512,1024]{1,0:T(8,128)(2,1)} custom-call(s32[1]{0:T(128)} %bitcast.23.role_ref, bf16[64,512]{1,0:T(8,128)(2,1)} %convolution_convert_fusion.3.left_ref, bf16[64,1024]{1,0:T(8,128)(2,1)} %get-tuple-element.38.right_ref, bf16[512,6144]{1,0:T(8,128)(2,1)} %w_ref.7, bf16[512,2048]{1,0:T(8,128)(2,1)} %collective-permute-done.25.m_ref.v_ref, ...), custom_call_target="tpu_custom_call" | custom-call | flops 67108864 | bytes 4194304 | tf_op jit(solution)/shard_map/update/pallas_call | solution.py:200
  146.9 2.0 %collective-permute-done.28.refs_6_ = bf16[512,512]{1,0:T(8,128)(2,1)} collective-permute-done((bf16[512,512]{1,0:T(8,128)(2,1)}, bf16[512,512]{1,0:T(8,128)(2,1)}, u32[]{:S(2)}, u32[]{:S(2)}) %collective-permute-start.28) | collective-permute-done | bytes 524320 | tf_op jit(solution)/shard_map/ppermute | solution.py:298
  149.9 3.4 %update.9.refs_10_ = bf16[512,512]{1,0:T(8,128)(2,1)} custom-call(s32[1]{0:T(128)} %bitcast.23.role_ref, bf16[64,512]{1,0:T(8,128)(2,1)} %get-tuple-element.42.left_ref, bf16[64,512]{1,0:T(8,128)(2,1)} %broadcast_select_fusion.1.right_ref, bf16[2048,512]{1,0:T(8,128)(2,1)} %w_ref.9, bf16[1024,512]{1,0:T(8,128)(2,1)} %copy-done.2, bf16[1024,512]{1,0:T(8,128)(2,1)} %copy-done.2), custom_call_target="tpu_custom_call" | custom-call | flops 33554432 | bytes 2097152 | tf_op jit(solution)/shard_map/update/pallas_call | solution.py:200
  153.9 2.2 %convolution_convert_fusion = bf16[64,512]{1,0:T(8,128)(2,1)} fusion(bf16[64,2048]{1,0:T(8,128)(2,1)} %get-tuple-element.32, bf16[2048,512]{1,0:T(8,128)(2,1)S(1)} %copy-done.1, s32[64]{0:T(128)S(1)} %iota_xor_fusion), kind=kOutput, calls=%fused_computation.16 | convolution fusion | flops 138481664 | bytes 2425088 | tf_op jit(solution)/shard_map/dot_general | solution.py:295
  156.1 0.8 copy-done.8
  156.9 5.7 %join.1 = (bf16[512,6144]{1,0:T(8,128)(2,1)}, bf16[4,512,512]{2,1,0:T(8,128)(2,1)}) custom-call(s32[1]{0:T(128)} %bitcast.23.role_ref, bf16[512,1024]{1,0:T(8,128)(2,1)} %get-tuple-element.37.refs_0_, bf16[512,1024]{1,0:T(8,128)(2,1)} %collective-permute-done.24.refs_1_, bf16[512,1024]{1,0:T(8,128)(2,1)} %update.7.refs_2_, ...), custom_call_target="tpu_custom_call" | custom-call | bytes 16777216 | tf_op jit(solution)/shard_map/join/pallas_call | solution.py:237
  (116 shorter events, 11.3 us)
Async XLA Ops:
  0.6 20.0 %copy-start = (bf16[256,512]{1,0:T(8,128)(2,1)S(1)}, bf16[256,512]{1,0:T(8,128)(2,1)}, u32[]{:S(2)}) copy-start(bf16[256,512]{1,0:T(8,128)(2,1)} %param.14) | copy-start | bytes 786436
  0.6 15.5 %copy-start.22 = (s32[1,8]{1,0:T(1,128)S(1)}, s32[1,8]{1,0:T(1,128)}, u32[]{:S(2)}) copy-start(s32[1,8]{1,0:T(1,128)} %param.12) | copy-start | bytes 100
  0.7 15.5 %collective-permute-start.6 = (s32[1,8]{1,0:T(1,128)}, s32[1,8]{1,0:T(1,128)S(1)}, u32[]{:S(2)}, u32[]{:S(2)}) collective-permute-start(s32[1,8]{1,0:T(1,128)} %param.12), channel_id=1, source_target_pairs={{0,7},{1,6},{2,5},{3,4},{4,3},{5,2},{6,1},{7,0},{8,15},{9,14},{10,... | collective-permute-start | bytes 104 | tf_op jit(solution)/shard_map/ppermute | solution.py:286
  6.8 10.2 %collective-permute-start.5 = (s32[1,8]{1,0:T(1,128)}, s32[1,8]{1,0:T(1,128)S(1)}, u32[]{:S(2)}, u32[]{:S(2)}) collective-permute-start(s32[1,8]{1,0:T(1,128)} %param.12), channel_id=1, source_target_pairs={{0,6},{1,7},{2,4},{3,5},{4,2},{5,3},{6,0},{7,1},{8,14},{9,15},{10,... | collective-permute-start | bytes 104 | tf_op jit(solution)/shard_map/ppermute | solution.py:286
  7.0 10.4 %collective-permute-start.4 = (s32[1,8]{1,0:T(1,128)}, s32[1,8]{1,0:T(1,128)S(1)}, u32[]{:S(2)}, u32[]{:S(2)}) collective-permute-start(s32[1,8]{1,0:T(1,128)} %param.12), channel_id=1, source_target_pairs={{0,5},{1,4},{2,7},{3,6},{4,1},{5,0},{6,3},{7,2},{8,13},{9,12},{10,... | collective-permute-start | bytes 104 | tf_op jit(solution)/shard_map/ppermute | solution.py:286
  7.7 9.7 %collective-permute-start.3 = (s32[1,8]{1,0:T(1,128)}, s32[1,8]{1,0:T(1,128)S(1)}, u32[]{:S(2)}, u32[]{:S(2)}) collective-permute-start(s32[1,8]{1,0:T(1,128)} %param.12), channel_id=1, source_target_pairs={{0,4},{1,5},{2,6},{3,7},{4,0},{5,1},{6,2},{7,3},{8,12},{9,13},{10,... | collective-permute-start | bytes 104 | tf_op jit(solution)/shard_map/ppermute | solution.py:286
  9.8 7.7 %collective-permute-start.2 = (s32[1,8]{1,0:T(1,128)}, s32[1,8]{1,0:T(1,128)S(1)}, u32[]{:S(2)}, u32[]{:S(2)}) collective-permute-start(s32[1,8]{1,0:T(1,128)} %param.12), channel_id=1, source_target_pairs={{0,3},{1,2},{2,1},{3,0},{4,7},{5,6},{6,5},{7,4},{8,11},{9,10},{10,... | collective-permute-start | bytes 104 | tf_op jit(solution)/shard_map/ppermute | solution.py:286
  16.1 3.6 %collective-permute-start.1 = (s32[1,8]{1,0:T(1,128)S(1)}, s32[1,8]{1,0:T(1,128)S(1)}, u32[]{:S(2)}, u32[]{:S(2)}) collective-permute-start(s32[1,8]{1,0:T(1,128)S(1)} %copy-done.22), channel_id=1, source_target_pairs={{0,2},{1,3},{2,0},{3,1},{4,6},{5,7},{6,4},{7,5},{8,10},{9,11},{10,... | collective-permute-start | bytes 104 | tf_op jit(solution)/shard_map/ppermute | solution.py:286
  17.0 3.6 %collective-permute-start = (s32[1,8]{1,0:T(1,128)S(1)}, s32[1,8]{1,0:T(1,128)S(1)}, u32[]{:S(2)}, u32[]{:S(2)}) collective-permute-start(s32[1,8]{1,0:T(1,128)S(1)} %copy-done.22), channel_id=1, source_target_pairs={{0,1},{1,0},{2,3},{3,2},{4,5},{5,4},{6,7},{7,6},{8,9},{9,8},{10,11... | collective-permute-start | bytes 104 | tf_op jit(solution)/shard_map/ppermute | solution.py:286
  24.8 19.9 %copy-start.3 = (f32[512,512]{1,0:T(8,128)S(1)}, f32[512,512]{1,0:T(8,128)}, u32[]{:S(2)}) copy-start(f32[512,512]{1,0:T(8,128)} %m_ref.5) | copy-start | bytes 3145732
  25.8 8.1 %collective-permute-start.7 = (bf16[8,8192]{1,0:T(8,128)(2,1)S(1)}, bf16[8,8192]{1,0:T(8,128)(2,1)S(1)}, u32[]{:S(2)}, u32[]{:S(2)}) collective-permute-start(bf16[8,8192]{1,0:T(8,128)(2,1)S(1)} %get-tuple-element.49), channel_id=1, source_target_pairs={{0,1},{1,0},{2,3},{3,2},{4,5},{5,4},{6,7},{7,6},{8,9},{9,8},{10,11... | collective-permute-start | bytes 393224 | tf_op jit(solution)/shard_map/ppermute | solution.py:286
  26.2 10.0 %collective-permute-start.13 = (bf16[8,8192]{1,0:T(8,128)(2,1)S(1)}, bf16[8,8192]{1,0:T(8,128)(2,1)S(1)}, u32[]{:S(2)}, u32[]{:S(2)}) collective-permute-start(bf16[8,8192]{1,0:T(8,128)(2,1)S(1)} %get-tuple-element.50), channel_id=1, source_target_pairs={{0,7},{1,6},{2,5},{3,4},{4,3},{5,2},{6,1},{7,0},{8,15},{9,14},{10,... | collective-permute-start | bytes 393224 | tf_op jit(solution)/shard_map/ppermute | solution.py:286
  30.9 18.6 %collective-permute-start.12 = (bf16[8,8192]{1,0:T(8,128)(2,1)}, bf16[8,8192]{1,0:T(8,128)(2,1)}, u32[]{:S(2)}, u32[]{:S(2)}) collective-permute-start(bf16[8,8192]{1,0:T(8,128)(2,1)} %get-tuple-element.51), channel_id=1, source_target_pairs={{0,6},{1,7},{2,4},{3,5},{4,2},{5,3},{6,0},{7,1},{8,14},{9,15},{10,... | collective-permute-start | bytes 393224 | tf_op jit(solution)/shard_map/ppermute | solution.py:286
  31.1 18.4 %collective-permute-start.11 = (bf16[8,8192]{1,0:T(8,128)(2,1)}, bf16[8,8192]{1,0:T(8,128)(2,1)}, u32[]{:S(2)}, u32[]{:S(2)}) collective-permute-start(bf16[8,8192]{1,0:T(8,128)(2,1)} %get-tuple-element.52), channel_id=1, source_target_pairs={{0,5},{1,4},{2,7},{3,6},{4,1},{5,0},{6,3},{7,2},{8,13},{9,12},{10,... | collective-permute-start | bytes 393224 | tf_op jit(solution)/shard_map/ppermute | solution.py:286
  31.5 19.6 %collective-permute-start.10 = (bf16[8,8192]{1,0:T(8,128)(2,1)}, bf16[8,8192]{1,0:T(8,128)(2,1)}, u32[]{:S(2)}, u32[]{:S(2)}) collective-permute-start(bf16[8,8192]{1,0:T(8,128)(2,1)} %get-tuple-element.53), channel_id=1, source_target_pairs={{0,4},{1,5},{2,6},{3,7},{4,0},{5,1},{6,2},{7,3},{8,12},{9,13},{10,... | collective-permute-start | bytes 393224 | tf_op jit(solution)/shard_map/ppermute | solution.py:286
  33.9 17.2 %collective-permute-start.9 = (bf16[8,8192]{1,0:T(8,128)(2,1)}, bf16[8,8192]{1,0:T(8,128)(2,1)}, u32[]{:S(2)}, u32[]{:S(2)}) collective-permute-start(bf16[8,8192]{1,0:T(8,128)(2,1)} %get-tuple-element.54), channel_id=1, source_target_pairs={{0,3},{1,2},{2,1},{3,0},{4,7},{5,6},{6,5},{7,4},{8,11},{9,10},{10,... | collective-permute-start | bytes 393224 | tf_op jit(solution)/shard_map/ppermute | solution.py:286
  36.9 14.4 %collective-permute-start.8 = (bf16[8,8192]{1,0:T(8,128)(2,1)}, bf16[8,8192]{1,0:T(8,128)(2,1)}, u32[]{:S(2)}, u32[]{:S(2)}) collective-permute-start(bf16[8,8192]{1,0:T(8,128)(2,1)} %get-tuple-element.55), channel_id=1, source_target_pairs={{0,2},{1,3},{2,0},{3,1},{4,6},{5,7},{6,4},{7,5},{8,10},{9,11},{10,... | collective-permute-start | bytes 393224 | tf_op jit(solution)/shard_map/ppermute | solution.py:286
  49.4 3.9 %copy-start.6 = (bf16[1,128,2048]{2,1,0:T(8,128)(2,1)S(1)}, bf16[1,128,2048]{2,1,0:T(8,128)(2,1)}, u32[]{:S(2)}) copy-start(bf16[1,128,2048]{2,1,0:T(8,128)(2,1)} %param.15) | copy-start | bytes 1572868
  49.4 3.9 %copy-start.7 = (bf16[1,128,2048]{2,1,0:T(8,128)(2,1)S(1)}, bf16[1,128,2048]{2,1,0:T(8,128)(2,1)}, u32[]{:S(2)}) copy-start(bf16[1,128,2048]{2,1,0:T(8,128)(2,1)} %param.16) | copy-start | bytes 1572868
  49.5 12.5 %collective-permute-start.30 = (bf16[64,512]{1,0:T(8,128)(2,1)S(1)}, bf16[64,512]{1,0:T(8,128)(2,1)S(1)}, u32[]{:S(2)}, u32[]{:S(2)}) collective-permute-start(bf16[64,512]{1,0:T(8,128)(2,1)S(1)} %convolution_convert_fusion.2), channel_id=1, source_target_pairs={{0,8},{8,0},{16,24},{24,16},{1,9},{9,1},{17,25},{25,17},{2,10},{10... | collective-permute-start | bytes 196616 | tf_op jit(solution)/shard_map/ppermute | solution.py:298
  49.5 92.0 %collective-permute-start.25 = (bf16[512,2048]{1,0:T(8,128)(2,1)}, bf16[512,2048]{1,0:T(8,128)(2,1)}, u32[]{:S(2)}, u32[]{:S(2)}) collective-permute-start(bf16[512,2048]{1,0:T(8,128)(2,1)} %pack.1), channel_id=1, source_target_pairs={{0,16},{8,24},{16,0},{24,8},{1,17},{9,25},{17,1},{25,9},{2,18},{10... | collective-permute-start | bytes 6291464 | tf_op jit(solution)/shard_map/ppermute | solution.py:298
  54.3 52.0 %copy-start.5 = (bf16[512,512]{1,0:T(8,128)(2,1)S(1)}, bf16[512,512]{1,0:T(8,128)(2,1)}, u32[]{:S(2)}) copy-start(bf16[512,512]{1,0:T(8,128)(2,1)} %convert_element_type.126) | copy-start | bytes 1572868
  59.4 39.2 %collective-permute-start.14 = (bf16[8,3712]{1,0:T(8,128)(2,1)}, bf16[8,3712]{1,0:T(8,128)(2,1)S(1)}, u32[]{:S(2)}, u32[]{:S(2)}) collective-permute-start(bf16[8,3712]{1,0:T(8,128)(2,1)} %get-tuple-element.29), channel_id=1, source_target_pairs={{24,0},{25,1},{26,2},{27,3},{28,4},{29,5},{30,6},{31,7}} | collective-permute-start | bytes 178184 | tf_op jit(solution)/shard_map/ppermute | solution.py:360
  60.6 37.9 %collective-permute-start.15 = (bf16[8,3712]{1,0:T(8,128)(2,1)}, bf16[8,3712]{1,0:T(8,128)(2,1)S(1)}, u32[]{:S(2)}, u32[]{:S(2)}) collective-permute-start(bf16[8,3712]{1,0:T(8,128)(2,1)} %get-tuple-element.30), channel_id=1, source_target_pairs={{24,8},{25,9},{26,10},{27,11},{28,12},{29,13},{30,14},{31,15}} | collective-permute-start | bytes 178184 | tf_op jit(solution)/shard_map/ppermute | solution.py:360
  61.3 37.2 %collective-permute-start.16 = (bf16[8,3712]{1,0:T(8,128)(2,1)}, bf16[8,3712]{1,0:T(8,128)(2,1)S(1)}, u32[]{:S(2)}, u32[]{:S(2)}) collective-permute-start(bf16[8,3712]{1,0:T(8,128)(2,1)} %get-tuple-element.31), channel_id=1, source_target_pairs={{24,16},{25,17},{26,18},{27,19},{28,20},{29,21},{30,22},{31,23}} | collective-permute-start | bytes 178184 | tf_op jit(solution)/shard_map/ppermute | solution.py:360
  62.0 41.3 %collective-permute-start.31 = (bf16[64,512]{1,0:T(8,128)(2,1)S(1)}, bf16[64,512]{1,0:T(8,128)(2,1)S(1)}, u32[]{:S(2)}, u32[]{:S(2)}) collective-permute-start(bf16[64,512]{1,0:T(8,128)(2,1)S(1)} %broadcast_select_fusion), channel_id=1, source_target_pairs={{0,16},{8,24},{16,0},{24,8},{1,17},{9,25},{17,1},{25,9},{2,18},{10... | collective-permute-start | bytes 196616 | tf_op jit(solution)/shard_map/ppermute | solution.py:298
  98.6 24.4 %copy-start.11 = (bf16[8,5760]{1,0:T(8,128)(2,1)}, bf16[8,5760]{1,0:T(8,128)(2,1)S(1)}, u32[]{:S(2)}) copy-start(bf16[8,5760]{1,0:T(8,128)(2,1)S(1)} %pad_maximum_fusion.3.refs_0_) | copy-start | bytes 276484
  98.6 8.0 %collective-permute-start.23 = (bf16[8,5760]{1,0:T(8,128)(2,1)S(1)}, bf16[8,5760]{1,0:T(8,128)(2,1)S(1)}, u32[]{:S(2)}, u32[]{:S(2)}) collective-permute-start(bf16[8,5760]{1,0:T(8,128)(2,1)S(1)} %pad_maximum_fusion.3.refs_0_), channel_id=1, source_target_pairs={{0,7},{1,6},{2,5},{3,4},{4,3},{5,2},{6,1},{7,0},{8,15},{9,14},{10,... | collective-permute-start | bytes 276488 | tf_op jit(solution)/shard_map/ppermute | solution.py:286
  102.2 7.3 %collective-permute-start.22 = (bf16[8,5760]{1,0:T(8,128)(2,1)S(1)}, bf16[8,5760]{1,0:T(8,128)(2,1)S(1)}, u32[]{:S(2)}, u32[]{:S(2)}) collective-permute-start(bf16[8,5760]{1,0:T(8,128)(2,1)S(1)} %pad_maximum_fusion.3.refs_0_), channel_id=1, source_target_pairs={{0,6},{1,7},{2,4},{3,5},{4,2},{5,3},{6,0},{7,1},{8,14},{9,15},{10,... | collective-permute-start | bytes 276488 | tf_op jit(solution)/shard_map/ppermute | solution.py:286
  103.3 12.8 %collective-permute-start.21 = (bf16[8,5760]{1,0:T(8,128)(2,1)S(1)}, bf16[8,5760]{1,0:T(8,128)(2,1)S(1)}, u32[]{:S(2)}, u32[]{:S(2)}) collective-permute-start(bf16[8,5760]{1,0:T(8,128)(2,1)S(1)} %pad_maximum_fusion.3.refs_0_), channel_id=1, source_target_pairs={{0,5},{1,4},{2,7},{3,6},{4,1},{5,0},{6,3},{7,2},{8,13},{9,12},{10,... | collective-permute-start | bytes 276488 | tf_op jit(solution)/shard_map/ppermute | solution.py:286
  103.3 14.9 %collective-permute-start.20 = (bf16[8,5760]{1,0:T(8,128)(2,1)S(1)}, bf16[8,5760]{1,0:T(8,128)(2,1)S(1)}, u32[]{:S(2)}, u32[]{:S(2)}) collective-permute-start(bf16[8,5760]{1,0:T(8,128)(2,1)S(1)} %pad_maximum_fusion.3.refs_0_), channel_id=1, source_target_pairs={{0,4},{1,5},{2,6},{3,7},{4,0},{5,1},{6,2},{7,3},{8,12},{9,13},{10,... | collective-permute-start | bytes 276488 | tf_op jit(solution)/shard_map/ppermute | solution.py:286
  106.6 16.4 %copy-start.14 = (bf16[8,5760]{1,0:T(8,128)(2,1)}, bf16[8,5760]{1,0:T(8,128)(2,1)S(1)}, u32[]{:S(2)}) copy-start(bf16[8,5760]{1,0:T(8,128)(2,1)S(1)} %collective-permute-done.23.refs_7_) | copy-start | bytes 276484
  106.6 42.3 %collective-permute-start.33 = (bf16[1024,512]{1,0:T(8,128)(2,1)S(1)}, bf16[1024,512]{1,0:T(8,128)(2,1)S(1)}, u32[]{:S(2)}, u32[]{:S(2)}) collective-permute-start(bf16[1024,512]{1,0:T(8,128)(2,1)S(1)} %pad_maximum_fusion.1), channel_id=1, source_target_pairs={{0,16},{8,24},{16,0},{24,8},{1,17},{9,25},{17,1},{25,9},{2,18},{10... | collective-permute-start | bytes 3145736 | tf_op jit(solution)/shard_map/ppermute | solution.py:298
  109.6 13.5 %copy-start.15 = (bf16[8,5760]{1,0:T(8,128)(2,1)}, bf16[8,5760]{1,0:T(8,128)(2,1)S(1)}, u32[]{:S(2)}) copy-start(bf16[8,5760]{1,0:T(8,128)(2,1)S(1)} %collective-permute-done.22.refs_6_) | copy-start | bytes 276484
  109.6 10.8 %collective-permute-start.19 = (bf16[8,5760]{1,0:T(8,128)(2,1)S(1)}, bf16[8,5760]{1,0:T(8,128)(2,1)S(1)}, u32[]{:S(2)}, u32[]{:S(2)}) collective-permute-start(bf16[8,5760]{1,0:T(8,128)(2,1)S(1)} %pad_maximum_fusion.3.refs_0_), channel_id=1, source_target_pairs={{0,3},{1,2},{2,1},{3,0},{4,7},{5,6},{6,5},{7,4},{8,11},{9,10},{10,... | collective-permute-start | bytes 276488 | tf_op jit(solution)/shard_map/ppermute | solution.py:286
  116.1 6.9 %copy-start.16 = (bf16[8,5760]{1,0:T(8,128)(2,1)}, bf16[8,5760]{1,0:T(8,128)(2,1)S(1)}, u32[]{:S(2)}) copy-start(bf16[8,5760]{1,0:T(8,128)(2,1)S(1)} %collective-permute-done.21.refs_5_) | copy-start | bytes 276484
  116.1 6.1 %collective-permute-start.18 = (bf16[8,5760]{1,0:T(8,128)(2,1)S(1)}, bf16[8,5760]{1,0:T(8,128)(2,1)S(1)}, u32[]{:S(2)}, u32[]{:S(2)}) collective-permute-start(bf16[8,5760]{1,0:T(8,128)(2,1)S(1)} %pad_maximum_fusion.3.refs_0_), channel_id=1, source_target_pairs={{0,2},{1,3},{2,0},{3,1},{4,6},{5,7},{6,4},{7,5},{8,10},{9,11},{10,... | collective-permute-start | bytes 276488 | tf_op jit(solution)/shard_map/ppermute | solution.py:286
  118.2 4.8 %copy-start.17 = (bf16[8,5760]{1,0:T(8,128)(2,1)}, bf16[8,5760]{1,0:T(8,128)(2,1)S(1)}, u32[]{:S(2)}) copy-start(bf16[8,5760]{1,0:T(8,128)(2,1)S(1)} %collective-permute-done.20.refs_4_) | copy-start | bytes 276484
  118.2 4.8 %collective-permute-start.17 = (bf16[8,5760]{1,0:T(8,128)(2,1)S(1)}, bf16[8,5760]{1,0:T(8,128)(2,1)S(1)}, u32[]{:S(2)}, u32[]{:S(2)}) collective-permute-start(bf16[8,5760]{1,0:T(8,128)(2,1)S(1)} %pad_maximum_fusion.3.refs_0_), channel_id=1, source_target_pairs={{0,1},{1,0},{2,3},{3,2},{4,5},{5,4},{6,7},{7,6},{8,9},{9,8},{10,11... | collective-permute-start | bytes 276488 | tf_op jit(solution)/shard_map/ppermute | solution.py:286
  125.8 3.8 %copy-start.21 = (bf16[64,128]{1,0:T(8,128)(2,1)S(1)}, bf16[64,128]{1,0:T(8,128)(2,1)}, u32[]{:S(2)}) copy-start(bf16[64,128]{1,0:T(8,128)(2,1)} %get-tuple-element.33) | copy-start | bytes 49156
  129.5 23.8 %collective-permute-start.32 = (bf16[512,512]{1,0:T(8,128)(2,1)}, bf16[512,512]{1,0:T(8,128)(2,1)}, u32[]{:S(2)}, u32[]{:S(2)}) collective-permute-start(bf16[512,512]{1,0:T(8,128)(2,1)} %get-tuple-element.41.refs_8_), channel_id=1, source_target_pairs={{0,8},{8,0},{16,24},{24,16},{1,9},{9,1},{17,25},{25,17},{2,10},{10... | collective-permute-start | bytes 1572872 | tf_op jit(solution)/shard_map/ppermute | solution.py:298
  134.3 14.6 %collective-permute-start.28 = (bf16[512,512]{1,0:T(8,128)(2,1)}, bf16[512,512]{1,0:T(8,128)(2,1)}, u32[]{:S(2)}, u32[]{:S(2)}) collective-permute-start(bf16[512,512]{1,0:T(8,128)(2,1)} %get-tuple-element.39.refs_4_), channel_id=1, source_target_pairs={{0,16},{8,24},{16,0},{24,8},{1,17},{9,25},{17,1},{25,9},{2,18},{10... | collective-permute-start | bytes 1572872 | tf_op jit(solution)/shard_map/ppermute | solution.py:298
  141.1 15.0 %collective-permute-start.24 = (bf16[512,1024]{1,0:T(8,128)(2,1)}, bf16[512,1024]{1,0:T(8,128)(2,1)}, u32[]{:S(2)}, u32[]{:S(2)}) collective-permute-start(bf16[512,1024]{1,0:T(8,128)(2,1)} %get-tuple-element.37.refs_0_), channel_id=1, source_target_pairs={{0,8},{8,0},{16,24},{24,16},{1,9},{9,1},{17,25},{25,17},{2,10},{10... | collective-permute-start | bytes 3145736 | tf_op jit(solution)/shard_map/ppermute | solution.py:298
  146.8 9.3 %collective-permute-start.26 = (bf16[512,1024]{1,0:T(8,128)(2,1)}, bf16[512,1024]{1,0:T(8,128)(2,1)}, u32[]{:S(2)}, u32[]{:S(2)}) collective-permute-start(bf16[512,1024]{1,0:T(8,128)(2,1)} %update.7.refs_2_), channel_id=1, source_target_pairs={{0,8},{8,0},{16,24},{24,16},{1,9},{9,1},{17,25},{25,17},{2,10},{10... | collective-permute-start | bytes 3145736 | tf_op jit(solution)/shard_map/ppermute | solution.py:298
  148.9 7.1 %collective-permute-start.27 = (bf16[512,512]{1,0:T(8,128)(2,1)}, bf16[512,512]{1,0:T(8,128)(2,1)}, u32[]{:S(2)}, u32[]{:S(2)}) collective-permute-start(bf16[512,512]{1,0:T(8,128)(2,1)} %get-tuple-element.39.refs_4_), channel_id=1, source_target_pairs={{0,8},{8,0},{16,24},{24,16},{1,9},{9,1},{17,25},{25,17},{2,10},{10... | collective-permute-start | bytes 1572872 | tf_op jit(solution)/shard_map/ppermute | solution.py:298
  148.9 7.1 %collective-permute-start.29 = (bf16[512,512]{1,0:T(8,128)(2,1)}, bf16[512,512]{1,0:T(8,128)(2,1)}, u32[]{:S(2)}, u32[]{:S(2)}) collective-permute-start(bf16[512,512]{1,0:T(8,128)(2,1)} %collective-permute-done.28.refs_6_), channel_id=1, source_target_pairs={{0,8},{8,0},{16,24},{24,16},{1,9},{9,1},{17,25},{25,17},{2,10},{10... | collective-permute-start | bytes 1572872 | tf_op jit(solution)/shard_map/ppermute | solution.py:298
  149.9 4.0 %copy-start.1 = (bf16[2048,512]{1,0:T(8,128)(2,1)S(1)}, bf16[2048,512]{1,0:T(8,128)(2,1)}, u32[]{:S(2)}) copy-start(bf16[2048,512]{1,0:T(8,128)(2,1)} %w_ref.9) | copy-start | bytes 6291460
  153.3 2.7 %collective-permute-start.34 = (bf16[512,512]{1,0:T(8,128)(2,1)}, bf16[512,512]{1,0:T(8,128)(2,1)S(1)}, u32[]{:S(2)}, u32[]{:S(2)}) collective-permute-start(bf16[512,512]{1,0:T(8,128)(2,1)} %update.9.refs_10_), channel_id=1, source_target_pairs={{0,8},{8,0},{16,24},{24,16},{1,9},{9,1},{17,25},{25,17},{2,10},{10... | collective-permute-start | bytes 1572872 | tf_op jit(solution)/shard_map/ppermute | solution.py:298
  (10 other events, 12.0 us)
where the time goes:
time: 163 us
  starting transfers between devices  51.6 us (32%)
  waiting for transfers between devices  50.7 us (31%)
  Pallas kernels  35.7 us (22%)
  matrix products  13.2 us (8%)
  local copies, waits for them, and re-layouts  5.71 us (4%)
  other arithmetic  4.18 us (3%)
  between operations  1.68 us (1%)
    ppermute x21, starting transfers between devices, hop(): return lax.ppermute(x, 'shard', [(i, i ^ k) for i in range(parts)])  44.2 us
    ppermute x3, waiting for transfers between devices, update(): got = lax.ppermute(parcels[q], 'role', [(learner, q)])  34.9 us
    pallas_call x5, Pallas kernels, update_blocks(): pl.pallas_call(functools.partial(update_body, len(aliases)), grid_spec=pl...  23 us
    ppermute x21, waiting for transfers between devices, hop(): return lax.ppermute(x, 'shard', [(i, i ^ k) for i in range(parts)])  13.7 us
    pallas_call x1, Pallas kernels, join(): pl.pallas_call(join_body, grid=(steps,), in_specs=[pl.BlockSpec(memory_sp...  5.73 us
    ppermute x11, starting transfers between devices, swap(): return lax.ppermute(x, 'role', [(i, i ^ bit) for i in range(roles)])  4.76 us
    dot_general x1, matrix products, update(): jnp.dot(inputs_of(ids), qkv_weight, preferred_element_type=f32)  4.16 us
    unnamed x48, local copies, waits for them, and re-layouts  4.12 us
  transfers between devices with their start and end apart: 35, of which 12 were waited for; matrix products, arithmetic and copies ran while one was open for 9% of the time, Pallas kernels for 18%

commit v1 on v0

--- a/solution.py
+++ b/solution.py
@@ -312,17 +312,23 @@
         ).astype(bf16)
         return jnp.dot(onehot, action_table, preferred_element_type=f32).astype(bf16)
 
+    inputs = inputs_of(ids)
     partial = jnp.concatenate(
-        [jnp.dot(inputs_of(ids), qkv_weight, preferred_element_type=f32), grad_partial], 1
+        [jnp.dot(inputs, qkv_weight, preferred_element_type=f32), grad_partial], 1
     )
     total = partial[:rows]
     pieces = partial[rows:].astype(bf16)
-    for k in range(1, parts):
-        total = total + hop(pieces[(k - 1) * rows : k * rows], k).astype(f32)
+    got = [hop(pieces[(k - 1) * rows : k * rows], k) for k in range(1, parts)]
+
+    side = jnp.concatenate([inputs, turned_cot], 1)
+    near_side = swap(side, 1)
+    near_side = jnp.where(is_learner, side, near_side)
+    near_side, got = lax.optimization_barrier((near_side, got))
+    far_side = swap(near_side, far)
+    for piece in got:
+        total = total + piece.astype(f32)
     total = total.astype(bf16)
 
-    near_cot = jnp.where(is_learner, turned_cot, swap(turned_cot, 1))
-    learner_cot = jnp.where(role >= far, near_cot, swap(near_cot, far))
 
     projected = total[:, : 3 * head_width].reshape(episodes, horizon, -1)
     grad_heads = total[:, 3 * head_width :]
@@ -342,7 +348,6 @@
         grad_heads.reshape(episodes, horizon, -1),
     ).reshape(rows, -1)
 
-    id_column = jnp.broadcast_to(action_ids.reshape(rows, 1).astype(bf16), (rows, 128))
 
     def wanted(q):
         own, other = q * qkv_part, (q ^ far) * qkv_part
@@ -351,10 +356,9 @@
             (0, other, other + early_width),
             (1, q * out_part, (q + 1) * out_part),
             (1, (q ^ far) * out_part, ((q ^ far) + 1) * out_part),
-            (2, 0, 128),
         )
 
-    parcels = parcel([grad_proj, masked_rows, id_column], tuple(wanted(q) for q in range(roles)))
+    parcels = parcel([grad_proj, masked_rows], tuple(wanted(q) for q in range(roles)))
     mine = None
     for q in range(learner):
         got = lax.ppermute(parcels[q], "role", [(learner, q)])
@@ -364,9 +368,11 @@
     moments_out = jnp.concatenate([first_out.astype(bf16), second_out.astype(bf16)], 0)
     far_moments_out = swap(moments_out, far)
     blocks = [mine] + [hop(mine, k) for k in range(1, parts)]
-    cuts = [qkv_part, early_width, out_part, out_part, 128, head_width]
-    own_rows, far_rows, own_mixed, far_mixed, learner_ids, gathered = stack(blocks, cuts)
-    learner_inputs = inputs_of(learner_ids[:, 0].astype(jnp.int32))
+    cuts = [qkv_part, early_width, out_part, out_part, head_width]
+    own_rows, far_rows, own_mixed, far_mixed, gathered = stack(blocks, cuts)
+    learner_side = jnp.where(role >= far, near_side, far_side)
+    learner_inputs = learner_side[:, : inputs.shape[1]]
+    learner_cot = learner_side[:, inputs.shape[1] :]
 
     third = qkv_part - early_width
     high = min(256, first_qkv.shape[0])

time: 163 us -> 174 us (1.067)
  waiting for transfers between devices: 50.7 us -> 68 us
  starting transfers between devices: 51.6 us -> 41.9 us
  other arithmetic: 4.18 us -> 8.54 us
    ppermute x11, waiting for transfers between devices: 2.06 us -> 38.7 us  [swap(): return lax.ppermute(x, 'role', [(i, i ^ bit) for i in range(roles)])]
    ppermute x3, waiting for transfers between devices: 34.9 us -> 0.01 us  [update(): got = lax.ppermute(parcels[q], 'role', [(learner, q)])]
    ppermute x21, waiting for transfers between devices: 13.7 us -> 29.3 us  [hop(): return lax.ppermute(x, 'shard', [(i, i ^ k) for i in range(parts)])]
    ppermute x21, starting transfers between devices: 44.2 us -> 31.8 us  [hop(): return lax.ppermute(x, 'shard', [(i, i ^ k) for i in range(parts)])]
    select_n x2, other arithmetic: 0.64 us -> 2.51 us  [the longest x1 1.59 us: update(): near_side = jnp.where(is_learner, side, near_side)]
    unnamed x48 -> x40, local copies, waits for them, and re-layouts: 4.12 us -> 3.62 us
  transfers between devices with their start and end apart: 35 -> 35, of which waited for: 12 -> 11; matrix products, arithmetic and copies ran while one was open for 9% -> 10% of each run, Pallas kernels for 18% -> 16%
where the time goes in v1:
time: 174 us; the launch traced here: 173 us
  waiting for transfers between devices  68 us (39%)
  starting transfers between devices  41.9 us (24%)
  Pallas kernels  35.6 us (20%)
  matrix products  12.4 us (7%)
  other arithmetic  8.54 us (5%)
  local copies, waits for them, and re-layouts  5.33 us (3%)
    ppermute x11, waiting for transfers between devices, swap(): return lax.ppermute(x, 'role', [(i, i ^ bit) for i in range(roles)])  38.7 us
    ppermute x21, starting transfers between devices, hop(): return lax.ppermute(x, 'shard', [(i, i ^ k) for i in range(parts)])  31.8 us
    ppermute x21, waiting for transfers between devices, hop(): return lax.ppermute(x, 'shard', [(i, i ^ k) for i in range(parts)])  29.3 us
    pallas_call x5, Pallas kernels, update_blocks(): pl.pallas_call(functools.partial(update_body, len(aliases)), grid_spec=pl...  23 us
    ppermute x11, starting transfers between devices, swap(): return lax.ppermute(x, 'role', [(i, i ^ bit) for i in range(roles)])  6.08 us
    pallas_call x1, Pallas kernels, join(): pl.pallas_call(join_body, grid=(steps,), in_specs=[pl.BlockSpec(memory_sp...  5.73 us
    dot_general x1, matrix products, update(): jnp.dot(inputs, qkv_weight, preferred_element_type=f32)  3.99 us
    ppermute x3, starting transfers between devices, update(): got = lax.ppermute(parcels[q], 'role', [(learner, q)])  3.97 us
  transfers between devices with their start and end apart: 35, of which 11 were waited for; matrix products, arithmetic and copies ran while one was open for 10% of the time, Pallas kernels for 16%

profile of v1, /device:TPU:0, one launch (start us, length us, event | category | flops | bytes accessed | tf_op | source)
XLA Modules:
  0.0 173.4 jit_solution(7820429889840619231)
XLA Ops:
  0.7 5.1 %collective-permute-start.5 = (s32[1,8]{1,0:T(1,128)}, s32[1,8]{1,0:T(1,128)S(1)}, u32[]{:S(2)}, u32[]{:S(2)}) collective-permute-start(s32[1,8]{1,0:T(1,128)} %param.12), channel_id=1, source_target_pairs={{0,6},{1,7},{2,4},{3,5},{4,2},{5,3},{6,0},{7,1},{8,14},{9,15},{10,... | collective-permute-start | bytes 104 | tf_op jit(solution)/shard_map/ppermute | solution.py:286
  6.2 3.5 %collective-permute-start.3 = (s32[1,8]{1,0:T(1,128)}, s32[1,8]{1,0:T(1,128)S(1)}, u32[]{:S(2)}, u32[]{:S(2)}) collective-permute-start(s32[1,8]{1,0:T(1,128)} %param.12), channel_id=1, source_target_pairs={{0,4},{1,5},{2,6},{3,7},{4,0},{5,1},{6,2},{7,3},{8,12},{9,13},{10,... | collective-permute-start | bytes 104 | tf_op jit(solution)/shard_map/ppermute | solution.py:286
  9.7 2.0 %collective-permute-start.1 = (s32[1,8]{1,0:T(1,128)}, s32[1,8]{1,0:T(1,128)S(1)}, u32[]{:S(2)}, u32[]{:S(2)}) collective-permute-start(s32[1,8]{1,0:T(1,128)} %param.12), channel_id=1, source_target_pairs={{0,2},{1,3},{2,0},{3,1},{4,6},{5,7},{6,4},{7,5},{8,10},{9,11},{10,... | collective-permute-start | bytes 104 | tf_op jit(solution)/shard_map/ppermute | solution.py:286
  12.9 1.0 convolution_convert_fusion.2
  13.9 2.3 %fusion.56 = f32[64,2048]{1,0:T(8,128)S(1)} fusion(bf16[64,512]{1,0:T(8,128)(2,1)S(1)} %convolution_convert_fusion.2, bf16[2048,512]{1,0:T(8,128)(2,1)} %w_ref.9), kind=kOutput, calls=%fused_computation.85 | convolution fusion | flops 134217728 | bytes 2686976 | tf_op jit(solution)/shard_map/dot_general | solution.py:305
  16.3 1.6 collective-permute-start
  17.9 2.0 %collective-permute-done = s32[1,8]{1,0:T(1,128)S(1)} collective-permute-done((s32[1,8]{1,0:T(1,128)S(1)}, s32[1,8]{1,0:T(1,128)S(1)}, u32[]{:S(2)}, u32[]{:S(2)}) %collective-permute-start) | collective-permute-done | bytes 64 | tf_op jit(solution)/shard_map/ppermute | solution.py:286
  19.9 4.2 %collective-permute-done.6 = s32[1,8]{1,0:T(1,128)S(1)} collective-permute-done((s32[1,8]{1,0:T(1,128)S(1)}, s32[1,8]{1,0:T(1,128)S(1)}, u32[]{:S(2)}, u32[]{:S(2)}) %collective-permute-start.6) | collective-permute-done | bytes 64 | tf_op jit(solution)/shard_map/ppermute | solution.py:286
  25.1 4.0 %fusion.55 = f32[64,6144]{1,0:T(8,128)S(1)} fusion(bf16[64,512]{1,0:T(8,128)(2,1)S(1)} %convolution_convert_fusion.3, bf16[512,6144]{1,0:T(8,128)(2,1)} %w_ref.7), kind=kOutput, calls=%fused_computation.84 | convolution fusion | flops 402653184 | bytes 7929856 | tf_op jit(solution)/shard_map/dot_general | solution.py:317
  29.2 0.9 fusion.48
  30.2 3.7 %collective-permute-start.13 = (bf16[8,8192]{1,0:T(8,128)(2,1)}, bf16[8,8192]{1,0:T(8,128)(2,1)}, u32[]{:S(2)}, u32[]{:S(2)}) collective-permute-start(bf16[8,8192]{1,0:T(8,128)(2,1)} %get-tuple-element.64), channel_id=1, source_target_pairs={{0,6},{1,7},{2,4},{3,5},{4,2},{5,3},{6,0},{7,1},{8,14},{9,15},{10,... | collective-permute-start | bytes 393224 | tf_op jit(solution)/shard_map/ppermute | solution.py:286
  34.0 3.9 %collective-permute-start.11 = (bf16[8,8192]{1,0:T(8,128)(2,1)}, bf16[8,8192]{1,0:T(8,128)(2,1)S(1)}, u32[]{:S(2)}, u32[]{:S(2)}) collective-permute-start(bf16[8,8192]{1,0:T(8,128)(2,1)} %get-tuple-element.66), channel_id=1, source_target_pairs={{0,4},{1,5},{2,6},{3,7},{4,0},{5,1},{6,2},{7,3},{8,12},{9,13},{10,... | collective-permute-start | bytes 393224 | tf_op jit(solution)/shard_map/ppermute | solution.py:286
  37.9 1.7 collective-permute-done.14
  39.9 1.6 collective-permute-done.13
  41.5 1.5 collective-permute-start.8
  43.0 1.6 broadcast_select_fusion.1
  44.6 7.5 %collective-permute-done.12 = bf16[8,8192]{1,0:T(8,128)(2,1)S(1)} collective-permute-done((bf16[8,8192]{1,0:T(8,128)(2,1)}, bf16[8,8192]{1,0:T(8,128)(2,1)S(1)}, u32[]{:S(2)}, u32[]{:S(2)}) %collective-permute-start.12) | collective-permute-done | bytes 131104 | tf_op jit(solution)/shard_map/ppermute | solution.py:286
  52.1 1.5 collective-permute-done.11
  53.6 1.1 fusion.30
  58.5 1.6 parcel.1
  60.1 1.3 collective-permute-start.15
  61.4 1.3 collective-permute-start.16
  62.6 1.4 collective-permute-start.17
  64.1 3.2 %pack.1 = bf16[512,2048]{1,0:T(8,128)(2,1)} custom-call(f32[512,1536]{1,0:T(8,128)} %first_ref.1, f32[512,1536]{1,0:T(8,128)} %second_ref.1), custom_call_target="tpu_custom_call" | custom-call | bytes 6291456 | tf_op jit(solution)/shard_map/pack/pallas_call | solution.py:91
  67.3 1.5 collective-permute-start.27
  69.0 1.1 collective-permute-start.25
  71.7 2.4 %collective-permute-start.24 = (bf16[8,5632]{1,0:T(8,128)(2,1)}, bf16[8,5632]{1,0:T(8,128)(2,1)}, u32[]{:S(2)}, u32[]{:S(2)}) collective-permute-start(bf16[8,5632]{1,0:T(8,128)(2,1)} %pad_maximum_fusion.4.refs_0_), channel_id=1, source_target_pairs={{0,7},{1,6},{2,5},{3,4},{4,3},{5,2},{6,1},{7,0},{8,15},{9,14},{10,... | collective-permute-start | bytes 270344 | tf_op jit(solution)/shard_map/ppermute | solution.py:286
  74.1 1.0 pad_maximum_fusion.1
  75.1 1.0 collective-permute-start.33
  76.1 2.4 %collective-permute-start.23 = (bf16[8,5632]{1,0:T(8,128)(2,1)}, bf16[8,5632]{1,0:T(8,128)(2,1)S(1)}, u32[]{:S(2)}, u32[]{:S(2)}) collective-permute-start(bf16[8,5632]{1,0:T(8,128)(2,1)} %pad_maximum_fusion.4.refs_0_), channel_id=1, source_target_pairs={{0,6},{1,7},{2,4},{3,5},{4,2},{5,3},{6,0},{7,1},{8,14},{9,15},{10,... | collective-permute-start | bytes 270344 | tf_op jit(solution)/shard_map/ppermute | solution.py:286
  78.5 38.6 %collective-permute-done.25 = bf16[64,1024]{1,0:T(8,128)(2,1)} collective-permute-done((bf16[64,1024]{1,0:T(8,128)(2,1)S(1)}, bf16[64,1024]{1,0:T(8,128)(2,1)}, u32[]{:S(2)}, u32[]{:S(2)}) %collective-permute-start.25) | collective-permute-done | bytes 131104 | tf_op jit(solution)/shard_map/ppermute | solution.py:298
  117.1 1.6 collective-permute-start.22
  118.7 2.2 %collective-permute-start.21 = (bf16[8,5632]{1,0:T(8,128)(2,1)}, bf16[8,5632]{1,0:T(8,128)(2,1)S(1)}, u32[]{:S(2)}, u32[]{:S(2)}) collective-permute-start(bf16[8,5632]{1,0:T(8,128)(2,1)} %pad_maximum_fusion.4.refs_0_), channel_id=1, source_target_pairs={{0,4},{1,5},{2,6},{3,7},{4,0},{5,1},{6,2},{7,3},{8,12},{9,13},{10,... | collective-permute-start | bytes 270344 | tf_op jit(solution)/shard_map/ppermute | solution.py:286
  120.9 0.9 broadcast_select_fusion
  122.6 3.0 %collective-permute-done.22.refs_5_ = bf16[8,5632]{1,0:T(8,128)(2,1)S(1)} collective-permute-done((bf16[8,5632]{1,0:T(8,128)(2,1)}, bf16[8,5632]{1,0:T(8,128)(2,1)S(1)}, u32[]{:S(2)}, u32[]{:S(2)}) %collective-permute-start.22) | collective-permute-done | bytes 90144 | tf_op jit(solution)/shard_map/ppermute | solution.py:286
  125.6 4.0 %collective-permute-done.21.refs_4_ = bf16[8,5632]{1,0:T(8,128)(2,1)S(1)} collective-permute-done((bf16[8,5632]{1,0:T(8,128)(2,1)}, bf16[8,5632]{1,0:T(8,128)(2,1)S(1)}, u32[]{:S(2)}, u32[]{:S(2)}) %collective-permute-start.21) | collective-permute-done | bytes 90144 | tf_op jit(solution)/shard_map/ppermute | solution.py:286
  130.7 1.1 collective-permute-done.19.refs_2_
  132.4 2.7 %collective-permute-done.18.refs_1_ = bf16[8,5632]{1,0:T(8,128)(2,1)} collective-permute-done((bf16[8,5632]{1,0:T(8,128)(2,1)}, bf16[8,5632]{1,0:T(8,128)(2,1)}, u32[]{:S(2)}, u32[]{:S(2)}) %collective-permute-start.18) | collective-permute-done | bytes 90144 | tf_op jit(solution)/shard_map/ppermute | solution.py:286
  135.2 2.1 %stack.1 = (bf16[64,1536]{1,0:T(8,128)(2,1)}, bf16[64,1024]{1,0:T(8,128)(2,1)}, bf16[64,512]{1,0:T(8,128)(2,1)}, bf16[64,512]{1,0:T(8,128)(2,1)}, bf16[64,2048]{1,0:T(8,128)(2,1)}) custom-call(bf16[8,5632]{1,0:T(8,128)(2,1)} %pad_maximum_fusion.4.refs_0_, bf16[8,5632]{1,0:T(8,128)(2,1)} %collective-permute-done.18.refs_1_, bf16[8,5632]{1,0:T(8,128)(2,1)} %copy-done.14, ...), custom_call_target="tpu_custom_call" | custom-call | tf_op jit(solution)/shard_map/stack/pallas_call | solution.py:113
  137.2 3.8 %update.8 = (bf16[512,512]{1,0:T(8,128)(2,1)}, f32[512,512]{1,0:T(8,128)}, f32[512,512]{1,0:T(8,128)}) custom-call(s32[1]{0:T(128)} %bitcast.22.role_ref, bf16[64,512]{1,0:T(8,128)(2,1)} %get-tuple-element.54.left_ref, bf16[64,512]{1,0:T(8,128)(2,1)} %get-tuple-element.70.right_ref, bf16[2048,512]{1,0:T(8,128)(2,1)} %w_ref.9, f32[512,512]{1,0:T(8,128)} %m_ref.5, ...), custom_call_target="tpu_custom_call" | custom-call | flops 33554432 | bytes 5242880 | tf_op jit(solution)/shard_map/update/pallas_call | solution.py:200
  141.0 3.8 %update.5 = (bf16[512,512]{1,0:T(8,128)(2,1)}, f32[512,1536]{1,0:T(8,128)}, f32[512,1536]{1,0:T(8,128)}) custom-call(s32[1]{0:T(128)} %bitcast.22.role_ref, bf16[64,512]{1,0:T(8,128)(2,1)} %get-tuple-element.71.left_ref, bf16[64,1536]{1,0:T(8,128)(2,1)} %get-tuple-element.48.right_ref, bf16[512,6144]{1,0:T(8,128)(2,1)} %w_ref.7, f32[512,1536]{1,0:T(8,128)} %first_ref.1, ...), custom_call_target="tpu_custom_call" | custom-call | flops 33554432 | bytes 5242880 | tf_op jit(solution)/shard_map/update/pallas_call | solution.py:200
  144.8 1.0 collective-permute-start.30
  145.8 6.7 %update.6 = (bf16[512,1024]{1,0:T(8,128)(2,1)}, f32[512,1536]{1,0:T(8,128)}, f32[512,1536]{1,0:T(8,128)}) custom-call(s32[1]{0:T(128)} %bitcast.22.role_ref, bf16[64,512]{1,0:T(8,128)(2,1)} %get-tuple-element.71.left_ref, bf16[64,1536]{1,0:T(8,128)(2,1)} %get-tuple-element.48.right_ref, ...), custom_call_target="tpu_custom_call", output_to_operand_aliasing={{1}: (6, {}), {2}: (7, {})} | custom-call | flops 67108864 | bytes 10485760 | tf_op jit(solution)/shard_map/update/pallas_call | solution.py:200
  152.6 1.3 copy-done.2
  153.9 5.3 %update.7.refs_2_ = bf16[512,1024]{1,0:T(8,128)(2,1)} custom-call(s32[1]{0:T(128)} %bitcast.22.role_ref, bf16[64,512]{1,0:T(8,128)(2,1)} %get-tuple-element.71.left_ref, bf16[64,1024]{1,0:T(8,128)(2,1)} %get-tuple-element.52.right_ref, bf16[512,6144]{1,0:T(8,128)(2,1)} %w_ref.7, bf16[512,2048]{1,0:T(8,128)(2,1)} %copy-done.2, bf16[512,2048]{1,0:T(8,128)(2,1)} %copy-done.2), custom_call_target="tpu_custom_call" | custom-call | flops 67108864 | bytes 4194304 | tf_op jit(solution)/shard_map/update/pallas_call | solution.py:200
  160.7 3.4 %update.9.refs_10_ = bf16[512,512]{1,0:T(8,128)(2,1)} custom-call(s32[1]{0:T(128)} %bitcast.22.role_ref, bf16[64,512]{1,0:T(8,128)(2,1)} %get-tuple-element.56.left_ref, bf16[64,512]{1,0:T(8,128)(2,1)} %get-tuple-element.70.right_ref, bf16[2048,512]{1,0:T(8,128)(2,1)} %w_ref.9, bf16[1024,512]{1,0:T(8,128)(2,1)} %copy-done.3, bf16[1024,512]{1,0:T(8,128)(2,1)} %copy-done.3), custom_call_target="tpu_custom_call" | custom-call | flops 33554432 | bytes 2097152 | tf_op jit(solution)/shard_map/update/pallas_call | solution.py:200
  164.6 2.2 %convolution_convert_fusion = bf16[64,512]{1,0:T(8,128)(2,1)} fusion(bf16[64,2048]{1,0:T(8,128)(2,1)} %get-tuple-element.46, bf16[2048,512]{1,0:T(8,128)(2,1)S(1)} %copy-done.1, s32[64]{0:T(128)S(1)} %iota_xor_fusion), kind=kOutput, calls=%fused_computation.16 | convolution fusion | flops 138481664 | bytes 2425088 | tf_op jit(solution)/shard_map/dot_general | solution.py:295
  167.7 5.7 %join.1 = (bf16[512,6144]{1,0:T(8,128)(2,1)}, bf16[4,512,512]{2,1,0:T(8,128)(2,1)}) custom-call(s32[1]{0:T(128)} %bitcast.22.role_ref, bf16[512,1024]{1,0:T(8,128)(2,1)} %get-tuple-element.51.refs_0_, bf16[512,1024]{1,0:T(8,128)(2,1)} %collective-permute-done.26.refs_1_, bf16[512,1024]{1,0:T(8,128)(2,1)} %update.7.refs_2_, ...), custom_call_target="tpu_custom_call" | custom-call | bytes 16777216 | tf_op jit(solution)/shard_map/join/pallas_call | solution.py:237
  (107 shorter events, 13.3 us)
Async XLA Ops:
  0.6 23.6 %copy-start = (bf16[256,512]{1,0:T(8,128)(2,1)S(1)}, bf16[256,512]{1,0:T(8,128)(2,1)}, u32[]{:S(2)}) copy-start(bf16[256,512]{1,0:T(8,128)(2,1)} %param.14) | copy-start | bytes 786436
  0.6 15.6 %copy-start.17 = (s32[1,8]{1,0:T(1,128)S(1)}, s32[1,8]{1,0:T(1,128)}, u32[]{:S(2)}) copy-start(s32[1,8]{1,0:T(1,128)} %param.12) | copy-start | bytes 100
  0.7 15.6 %collective-permute-start.5 = (s32[1,8]{1,0:T(1,128)}, s32[1,8]{1,0:T(1,128)S(1)}, u32[]{:S(2)}, u32[]{:S(2)}) collective-permute-start(s32[1,8]{1,0:T(1,128)} %param.12), channel_id=1, source_target_pairs={{0,6},{1,7},{2,4},{3,5},{4,2},{5,3},{6,0},{7,1},{8,14},{9,15},{10,... | collective-permute-start | bytes 104 | tf_op jit(solution)/shard_map/ppermute | solution.py:286
  5.8 12.0 %collective-permute-start.4 = (s32[1,8]{1,0:T(1,128)}, s32[1,8]{1,0:T(1,128)S(1)}, u32[]{:S(2)}, u32[]{:S(2)}) collective-permute-start(s32[1,8]{1,0:T(1,128)} %param.12), channel_id=1, source_target_pairs={{0,5},{1,4},{2,7},{3,6},{4,1},{5,0},{6,3},{7,2},{8,13},{9,12},{10,... | collective-permute-start | bytes 104 | tf_op jit(solution)/shard_map/ppermute | solution.py:286
  6.2 11.7 %collective-permute-start.3 = (s32[1,8]{1,0:T(1,128)}, s32[1,8]{1,0:T(1,128)S(1)}, u32[]{:S(2)}, u32[]{:S(2)}) collective-permute-start(s32[1,8]{1,0:T(1,128)} %param.12), channel_id=1, source_target_pairs={{0,4},{1,5},{2,6},{3,7},{4,0},{5,1},{6,2},{7,3},{8,12},{9,13},{10,... | collective-permute-start | bytes 104 | tf_op jit(solution)/shard_map/ppermute | solution.py:286
  9.7 8.2 %collective-permute-start.2 = (s32[1,8]{1,0:T(1,128)}, s32[1,8]{1,0:T(1,128)S(1)}, u32[]{:S(2)}, u32[]{:S(2)}) collective-permute-start(s32[1,8]{1,0:T(1,128)} %param.12), channel_id=1, source_target_pairs={{0,3},{1,2},{2,1},{3,0},{4,7},{5,6},{6,5},{7,4},{8,11},{9,10},{10,... | collective-permute-start | bytes 104 | tf_op jit(solution)/shard_map/ppermute | solution.py:286
  9.7 8.2 %collective-permute-start.1 = (s32[1,8]{1,0:T(1,128)}, s32[1,8]{1,0:T(1,128)S(1)}, u32[]{:S(2)}, u32[]{:S(2)}) collective-permute-start(s32[1,8]{1,0:T(1,128)} %param.12), channel_id=1, source_target_pairs={{0,2},{1,3},{2,0},{3,1},{4,6},{5,7},{6,4},{7,5},{8,10},{9,11},{10,... | collective-permute-start | bytes 104 | tf_op jit(solution)/shard_map/ppermute | solution.py:286
  16.3 3.6 %collective-permute-start = (s32[1,8]{1,0:T(1,128)S(1)}, s32[1,8]{1,0:T(1,128)S(1)}, u32[]{:S(2)}, u32[]{:S(2)}) collective-permute-start(s32[1,8]{1,0:T(1,128)S(1)} %copy-done.17), channel_id=1, source_target_pairs={{0,1},{1,0},{2,3},{3,2},{4,5},{5,4},{6,7},{7,6},{8,9},{9,8},{10,11... | collective-permute-start | bytes 104 | tf_op jit(solution)/shard_map/ppermute | solution.py:286
  17.9 6.3 %collective-permute-start.6 = (s32[1,8]{1,0:T(1,128)S(1)}, s32[1,8]{1,0:T(1,128)S(1)}, u32[]{:S(2)}, u32[]{:S(2)}) collective-permute-start(s32[1,8]{1,0:T(1,128)S(1)} %copy-done.17), channel_id=1, source_target_pairs={{0,7},{1,6},{2,5},{3,4},{4,3},{5,2},{6,1},{7,0},{8,15},{9,14},{10,... | collective-permute-start | bytes 104 | tf_op jit(solution)/shard_map/ppermute | solution.py:286
  25.1 12.8 %collective-permute-start.7 = (bf16[64,1024]{1,0:T(8,128)(2,1)}, bf16[64,1024]{1,0:T(8,128)(2,1)}, u32[]{:S(2)}, u32[]{:S(2)}) collective-permute-start(bf16[64,1024]{1,0:T(8,128)(2,1)} %pad_maximum_fusion.2), channel_id=1, source_target_pairs={{0,8},{8,0},{16,24},{24,16},{1,9},{9,1},{17,25},{25,17},{2,10},{10... | collective-permute-start | bytes 393224 | tf_op jit(solution)/shard_map/ppermute | solution.py:298
  29.1 4.8 %copy-start.18 = (pred[136]{0:T(512)(128)(4,1)S(1)}, pred[136]{0:T(512)(128)(4,1)}, u32[]{:S(2)}) copy-start(pred[136]{0:T(512)(128)(4,1)} %get-tuple-element.79) | copy-start | bytes 412
  30.1 24.6 %copy-start.6 = (bf16[1,128,2048]{2,1,0:T(8,128)(2,1)S(1)}, bf16[1,128,2048]{2,1,0:T(8,128)(2,1)}, u32[]{:S(2)}) copy-start(bf16[1,128,2048]{2,1,0:T(8,128)(2,1)} %param.15) | copy-start | bytes 1572868
  30.1 24.6 %copy-start.7 = (bf16[1,128,2048]{2,1,0:T(8,128)(2,1)S(1)}, bf16[1,128,2048]{2,1,0:T(8,128)(2,1)}, u32[]{:S(2)}) copy-start(bf16[1,128,2048]{2,1,0:T(8,128)(2,1)} %param.16) | copy-start | bytes 1572868
  30.1 9.5 %collective-permute-start.14 = (bf16[8,8192]{1,0:T(8,128)(2,1)}, bf16[8,8192]{1,0:T(8,128)(2,1)}, u32[]{:S(2)}, u32[]{:S(2)}) collective-permute-start(bf16[8,8192]{1,0:T(8,128)(2,1)} %get-tuple-element.63), channel_id=1, source_target_pairs={{0,7},{1,6},{2,5},{3,4},{4,3},{5,2},{6,1},{7,0},{8,15},{9,14},{10,... | collective-permute-start | bytes 393224 | tf_op jit(solution)/shard_map/ppermute | solution.py:286
  30.2 11.3 %collective-permute-start.13 = (bf16[8,8192]{1,0:T(8,128)(2,1)}, bf16[8,8192]{1,0:T(8,128)(2,1)}, u32[]{:S(2)}, u32[]{:S(2)}) collective-permute-start(bf16[8,8192]{1,0:T(8,128)(2,1)} %get-tuple-element.64), channel_id=1, source_target_pairs={{0,6},{1,7},{2,4},{3,5},{4,2},{5,3},{6,0},{7,1},{8,14},{9,15},{10,... | collective-permute-start | bytes 393224 | tf_op jit(solution)/shard_map/ppermute | solution.py:286
  34.0 18.2 %collective-permute-start.12 = (bf16[8,8192]{1,0:T(8,128)(2,1)}, bf16[8,8192]{1,0:T(8,128)(2,1)S(1)}, u32[]{:S(2)}, u32[]{:S(2)}) collective-permute-start(bf16[8,8192]{1,0:T(8,128)(2,1)} %get-tuple-element.65), channel_id=1, source_target_pairs={{0,5},{1,4},{2,7},{3,6},{4,1},{5,0},{6,3},{7,2},{8,13},{9,12},{10,... | collective-permute-start | bytes 393224 | tf_op jit(solution)/shard_map/ppermute | solution.py:286
  34.0 19.5 %collective-permute-start.11 = (bf16[8,8192]{1,0:T(8,128)(2,1)}, bf16[8,8192]{1,0:T(8,128)(2,1)S(1)}, u32[]{:S(2)}, u32[]{:S(2)}) collective-permute-start(bf16[8,8192]{1,0:T(8,128)(2,1)} %get-tuple-element.66), channel_id=1, source_target_pairs={{0,4},{1,5},{2,6},{3,7},{4,0},{5,1},{6,2},{7,3},{8,12},{9,13},{10,... | collective-permute-start | bytes 393224 | tf_op jit(solution)/shard_map/ppermute | solution.py:286
  37.9 15.7 %collective-permute-start.10 = (bf16[8,8192]{1,0:T(8,128)(2,1)}, bf16[8,8192]{1,0:T(8,128)(2,1)S(1)}, u32[]{:S(2)}, u32[]{:S(2)}) collective-permute-start(bf16[8,8192]{1,0:T(8,128)(2,1)} %get-tuple-element.67), channel_id=1, source_target_pairs={{0,3},{1,2},{2,1},{3,0},{4,7},{5,6},{6,5},{7,4},{8,11},{9,10},{10,... | collective-permute-start | bytes 393224 | tf_op jit(solution)/shard_map/ppermute | solution.py:286
  39.6 13.9 %collective-permute-start.9 = (bf16[8,8192]{1,0:T(8,128)(2,1)}, bf16[8,8192]{1,0:T(8,128)(2,1)S(1)}, u32[]{:S(2)}, u32[]{:S(2)}) collective-permute-start(bf16[8,8192]{1,0:T(8,128)(2,1)} %get-tuple-element.68), channel_id=1, source_target_pairs={{0,2},{1,3},{2,0},{3,1},{4,6},{5,7},{6,4},{7,5},{8,10},{9,11},{10,... | collective-permute-start | bytes 393224 | tf_op jit(solution)/shard_map/ppermute | solution.py:286
  41.5 12.1 %collective-permute-start.8 = (bf16[8,8192]{1,0:T(8,128)(2,1)}, bf16[8,8192]{1,0:T(8,128)(2,1)S(1)}, u32[]{:S(2)}, u32[]{:S(2)}) collective-permute-start(bf16[8,8192]{1,0:T(8,128)(2,1)} %get-tuple-element.69), channel_id=1, source_target_pairs={{0,1},{1,0},{2,3},{3,2},{4,5},{5,4},{6,7},{7,6},{8,9},{9,8},{10,11... | collective-permute-start | bytes 393224 | tf_op jit(solution)/shard_map/ppermute | solution.py:286
  60.1 10.1 %collective-permute-start.15 = (bf16[8,3584]{1,0:T(8,128)(2,1)}, bf16[8,3584]{1,0:T(8,128)(2,1)}, u32[]{:S(2)}, u32[]{:S(2)}) collective-permute-start(bf16[8,3584]{1,0:T(8,128)(2,1)} %get-tuple-element.43), channel_id=1, source_target_pairs={{24,0},{25,1},{26,2},{27,3},{28,4},{29,5},{30,6},{31,7}} | collective-permute-start | bytes 172040 | tf_op jit(solution)/shard_map/ppermute | solution.py:364
  61.4 8.8 %collective-permute-start.16 = (bf16[8,3584]{1,0:T(8,128)(2,1)}, bf16[8,3584]{1,0:T(8,128)(2,1)}, u32[]{:S(2)}, u32[]{:S(2)}) collective-permute-start(bf16[8,3584]{1,0:T(8,128)(2,1)} %get-tuple-element.44), channel_id=1, source_target_pairs={{24,8},{25,9},{26,10},{27,11},{28,12},{29,13},{30,14},{31,15}} | collective-permute-start | bytes 172040 | tf_op jit(solution)/shard_map/ppermute | solution.py:364
  62.6 6.2 %copy-start.4 = (f32[512,512]{1,0:T(8,128)S(1)}, f32[512,512]{1,0:T(8,128)}, u32[]{:S(2)}) copy-start(f32[512,512]{1,0:T(8,128)} %m_ref.5) | copy-start | bytes 3145732
  62.6 7.5 %collective-permute-start.17 = (bf16[8,3584]{1,0:T(8,128)(2,1)}, bf16[8,3584]{1,0:T(8,128)(2,1)}, u32[]{:S(2)}, u32[]{:S(2)}) collective-permute-start(bf16[8,3584]{1,0:T(8,128)(2,1)} %get-tuple-element.45), channel_id=1, source_target_pairs={{24,16},{25,17},{26,18},{27,19},{28,20},{29,21},{30,22},{31,23}} | collective-permute-start | bytes 172040 | tf_op jit(solution)/shard_map/ppermute | solution.py:364
  67.3 2.9 %copy-start.15 = (bf16[8,3584]{1,0:T(8,128)(2,1)S(1)}, bf16[8,3584]{1,0:T(8,128)(2,1)}, u32[]{:S(2)}) copy-start(bf16[8,3584]{1,0:T(8,128)(2,1)} %get-tuple-element.42) | copy-start | bytes 172036
  67.3 3.8 %copy-start.16 = (bf16[8,2048]{1,0:T(8,128)(2,1)S(1)}, bf16[8,2048]{1,0:T(8,128)(2,1)}, u32[]{:S(2)}) copy-start(bf16[8,2048]{1,0:T(8,128)(2,1)} %get-tuple-element.75) | copy-start | bytes 98308
  67.3 85.2 %collective-permute-start.27 = (bf16[512,2048]{1,0:T(8,128)(2,1)}, bf16[512,2048]{1,0:T(8,128)(2,1)S(1)}, u32[]{:S(2)}, u32[]{:S(2)}) collective-permute-start(bf16[512,2048]{1,0:T(8,128)(2,1)} %pack.1), channel_id=1, source_target_pairs={{0,16},{8,24},{16,0},{24,8},{1,17},{9,25},{17,1},{25,9},{2,18},{10... | collective-permute-start | bytes 6291464 | tf_op jit(solution)/shard_map/ppermute | solution.py:298
  69.0 48.1 %collective-permute-start.25 = (bf16[64,1024]{1,0:T(8,128)(2,1)S(1)}, bf16[64,1024]{1,0:T(8,128)(2,1)}, u32[]{:S(2)}, u32[]{:S(2)}) collective-permute-start(bf16[64,1024]{1,0:T(8,128)(2,1)S(1)} %copy-done.9), channel_id=1, source_target_pairs={{0,16},{8,24},{16,0},{24,8},{1,17},{9,25},{17,1},{25,9},{2,18},{10... | collective-permute-start | bytes 393224 | tf_op jit(solution)/shard_map/ppermute | solution.py:298
  71.7 47.0 %collective-permute-start.24 = (bf16[8,5632]{1,0:T(8,128)(2,1)}, bf16[8,5632]{1,0:T(8,128)(2,1)}, u32[]{:S(2)}, u32[]{:S(2)}) collective-permute-start(bf16[8,5632]{1,0:T(8,128)(2,1)} %pad_maximum_fusion.4.refs_0_), channel_id=1, source_target_pairs={{0,7},{1,6},{2,5},{3,4},{4,3},{5,2},{6,1},{7,0},{8,15},{9,14},{10,... | collective-permute-start | bytes 270344 | tf_op jit(solution)/shard_map/ppermute | solution.py:286
  75.1 84.6 %collective-permute-start.33 = (bf16[1024,512]{1,0:T(8,128)(2,1)}, bf16[1024,512]{1,0:T(8,128)(2,1)S(1)}, u32[]{:S(2)}, u32[]{:S(2)}) collective-permute-start(bf16[1024,512]{1,0:T(8,128)(2,1)} %pad_maximum_fusion.1), channel_id=1, source_target_pairs={{0,16},{8,24},{16,0},{24,8},{1,17},{9,25},{17,1},{25,9},{2,18},{10... | collective-permute-start | bytes 3145736 | tf_op jit(solution)/shard_map/ppermute | solution.py:298
  76.1 45.8 %collective-permute-start.23 = (bf16[8,5632]{1,0:T(8,128)(2,1)}, bf16[8,5632]{1,0:T(8,128)(2,1)S(1)}, u32[]{:S(2)}, u32[]{:S(2)}) collective-permute-start(bf16[8,5632]{1,0:T(8,128)(2,1)} %pad_maximum_fusion.4.refs_0_), channel_id=1, source_target_pairs={{0,6},{1,7},{2,4},{3,5},{4,2},{5,3},{6,0},{7,1},{8,14},{9,15},{10,... | collective-permute-start | bytes 270344 | tf_op jit(solution)/shard_map/ppermute | solution.py:286
  117.1 8.5 %collective-permute-start.22 = (bf16[8,5632]{1,0:T(8,128)(2,1)}, bf16[8,5632]{1,0:T(8,128)(2,1)S(1)}, u32[]{:S(2)}, u32[]{:S(2)}) collective-permute-start(bf16[8,5632]{1,0:T(8,128)(2,1)} %pad_maximum_fusion.4.refs_0_), channel_id=1, source_target_pairs={{0,5},{1,4},{2,7},{3,6},{4,1},{5,0},{6,3},{7,2},{8,13},{9,12},{10,... | collective-permute-start | bytes 270344 | tf_op jit(solution)/shard_map/ppermute | solution.py:286
  118.7 10.9 %collective-permute-start.21 = (bf16[8,5632]{1,0:T(8,128)(2,1)}, bf16[8,5632]{1,0:T(8,128)(2,1)S(1)}, u32[]{:S(2)}, u32[]{:S(2)}) collective-permute-start(bf16[8,5632]{1,0:T(8,128)(2,1)} %pad_maximum_fusion.4.refs_0_), channel_id=1, source_target_pairs={{0,4},{1,5},{2,6},{3,7},{4,0},{5,1},{6,2},{7,3},{8,12},{9,13},{10,... | collective-permute-start | bytes 270344 | tf_op jit(solution)/shard_map/ppermute | solution.py:286
  121.9 8.8 %copy-start.10 = (bf16[8,5632]{1,0:T(8,128)(2,1)}, bf16[8,5632]{1,0:T(8,128)(2,1)S(1)}, u32[]{:S(2)}) copy-start(bf16[8,5632]{1,0:T(8,128)(2,1)S(1)} %collective-permute-done.23.refs_6_) | copy-start | bytes 270340
  121.9 8.8 %collective-permute-start.20 = (bf16[8,5632]{1,0:T(8,128)(2,1)}, bf16[8,5632]{1,0:T(8,128)(2,1)S(1)}, u32[]{:S(2)}, u32[]{:S(2)}) collective-permute-start(bf16[8,5632]{1,0:T(8,128)(2,1)} %pad_maximum_fusion.4.refs_0_), channel_id=1, source_target_pairs={{0,3},{1,2},{2,1},{3,0},{4,7},{5,6},{6,5},{7,4},{8,11},{9,10},{10,... | collective-permute-start | bytes 270344 | tf_op jit(solution)/shard_map/ppermute | solution.py:286
  125.6 5.1 %copy-start.11 = (bf16[8,5632]{1,0:T(8,128)(2,1)}, bf16[8,5632]{1,0:T(8,128)(2,1)S(1)}, u32[]{:S(2)}) copy-start(bf16[8,5632]{1,0:T(8,128)(2,1)S(1)} %collective-permute-done.22.refs_5_) | copy-start | bytes 270340
  125.6 6.2 %collective-permute-start.19 = (bf16[8,5632]{1,0:T(8,128)(2,1)}, bf16[8,5632]{1,0:T(8,128)(2,1)S(1)}, u32[]{:S(2)}, u32[]{:S(2)}) collective-permute-start(bf16[8,5632]{1,0:T(8,128)(2,1)} %pad_maximum_fusion.4.refs_0_), channel_id=1, source_target_pairs={{0,2},{1,3},{2,0},{3,1},{4,6},{5,7},{6,4},{7,5},{8,10},{9,11},{10,... | collective-permute-start | bytes 270344 | tf_op jit(solution)/shard_map/ppermute | solution.py:286
  129.6 2.2 %copy-start.12 = (bf16[8,5632]{1,0:T(8,128)(2,1)}, bf16[8,5632]{1,0:T(8,128)(2,1)S(1)}, u32[]{:S(2)}) copy-start(bf16[8,5632]{1,0:T(8,128)(2,1)S(1)} %collective-permute-done.21.refs_4_) | copy-start | bytes 270340
  129.6 5.6 %collective-permute-start.18 = (bf16[8,5632]{1,0:T(8,128)(2,1)}, bf16[8,5632]{1,0:T(8,128)(2,1)}, u32[]{:S(2)}, u32[]{:S(2)}) collective-permute-start(bf16[8,5632]{1,0:T(8,128)(2,1)} %pad_maximum_fusion.4.refs_0_), channel_id=1, source_target_pairs={{0,1},{1,0},{2,3},{3,2},{4,5},{5,4},{6,7},{7,6},{8,9},{9,8},{10,11... | collective-permute-start | bytes 270344 | tf_op jit(solution)/shard_map/ppermute | solution.py:286
  130.7 4.4 %copy-start.13 = (bf16[8,5632]{1,0:T(8,128)(2,1)}, bf16[8,5632]{1,0:T(8,128)(2,1)S(1)}, u32[]{:S(2)}) copy-start(bf16[8,5632]{1,0:T(8,128)(2,1)S(1)} %collective-permute-done.20.refs_3_) | copy-start | bytes 270340
  141.0 23.1 %collective-permute-start.32 = (bf16[512,512]{1,0:T(8,128)(2,1)}, bf16[512,512]{1,0:T(8,128)(2,1)}, u32[]{:S(2)}, u32[]{:S(2)}) collective-permute-start(bf16[512,512]{1,0:T(8,128)(2,1)} %get-tuple-element.55.refs_8_), channel_id=1, source_target_pairs={{0,8},{8,0},{16,24},{24,16},{1,9},{9,1},{17,25},{25,17},{2,10},{10... | collective-permute-start | bytes 1572872 | tf_op jit(solution)/shard_map/ppermute | solution.py:298
  144.8 14.8 %collective-permute-start.30 = (bf16[512,512]{1,0:T(8,128)(2,1)}, bf16[512,512]{1,0:T(8,128)(2,1)}, u32[]{:S(2)}, u32[]{:S(2)}) collective-permute-start(bf16[512,512]{1,0:T(8,128)(2,1)} %get-tuple-element.53.refs_4_), channel_id=1, source_target_pairs={{0,16},{8,24},{16,0},{24,8},{1,17},{9,25},{17,1},{25,9},{2,18},{10... | collective-permute-start | bytes 1572872 | tf_op jit(solution)/shard_map/ppermute | solution.py:298
  152.5 14.3 %collective-permute-start.26 = (bf16[512,1024]{1,0:T(8,128)(2,1)}, bf16[512,1024]{1,0:T(8,128)(2,1)}, u32[]{:S(2)}, u32[]{:S(2)}) collective-permute-start(bf16[512,1024]{1,0:T(8,128)(2,1)} %get-tuple-element.51.refs_0_), channel_id=1, source_target_pairs={{0,8},{8,0},{16,24},{24,16},{1,9},{9,1},{17,25},{25,17},{2,10},{10... | collective-permute-start | bytes 3145736 | tf_op jit(solution)/shard_map/ppermute | solution.py:298
  159.2 7.7 %collective-permute-start.28 = (bf16[512,1024]{1,0:T(8,128)(2,1)}, bf16[512,1024]{1,0:T(8,128)(2,1)}, u32[]{:S(2)}, u32[]{:S(2)}) collective-permute-start(bf16[512,1024]{1,0:T(8,128)(2,1)} %update.7.refs_2_), channel_id=1, source_target_pairs={{0,8},{8,0},{16,24},{24,16},{1,9},{9,1},{17,25},{25,17},{2,10},{10... | collective-permute-start | bytes 3145736 | tf_op jit(solution)/shard_map/ppermute | solution.py:298
  159.6 7.1 %collective-permute-start.29 = (bf16[512,512]{1,0:T(8,128)(2,1)}, bf16[512,512]{1,0:T(8,128)(2,1)}, u32[]{:S(2)}, u32[]{:S(2)}) collective-permute-start(bf16[512,512]{1,0:T(8,128)(2,1)} %get-tuple-element.53.refs_4_), channel_id=1, source_target_pairs={{0,8},{8,0},{16,24},{24,16},{1,9},{9,1},{17,25},{25,17},{2,10},{10... | collective-permute-start | bytes 1572872 | tf_op jit(solution)/shard_map/ppermute | solution.py:298
  159.7 7.1 %collective-permute-start.31 = (bf16[512,512]{1,0:T(8,128)(2,1)}, bf16[512,512]{1,0:T(8,128)(2,1)}, u32[]{:S(2)}, u32[]{:S(2)}) collective-permute-start(bf16[512,512]{1,0:T(8,128)(2,1)} %collective-permute-done.30.refs_6_), channel_id=1, source_target_pairs={{0,8},{8,0},{16,24},{24,16},{1,9},{9,1},{17,25},{25,17},{2,10},{10... | collective-permute-start | bytes 1572872 | tf_op jit(solution)/shard_map/ppermute | solution.py:298
  160.7 3.9 %copy-start.1 = (bf16[2048,512]{1,0:T(8,128)(2,1)S(1)}, bf16[2048,512]{1,0:T(8,128)(2,1)}, u32[]{:S(2)}) copy-start(bf16[2048,512]{1,0:T(8,128)(2,1)} %w_ref.9) | copy-start | bytes 6291460
  164.1 2.7 %collective-permute-start.34 = (bf16[512,512]{1,0:T(8,128)(2,1)}, bf16[512,512]{1,0:T(8,128)(2,1)S(1)}, u32[]{:S(2)}, u32[]{:S(2)}) collective-permute-start(bf16[512,512]{1,0:T(8,128)(2,1)} %update.9.refs_10_), channel_id=1, source_target_pairs={{0,8},{8,0},{16,24},{24,16},{1,9},{9,1},{17,25},{25,17},{2,10},{10... | collective-permute-start | bytes 1572872 | tf_op jit(solution)/shard_map/ppermute | solution.py:298
  (6 other events, 7.2 us)
